TPU v7x, 256 devices: a whole 4x4x8 slice. The times are simulated.
256 devices in a mesh: ctx: 64 (over z, x, core), fsdp: 4 (over y).
Axes of the slice: x: 4, y: 4, z: 8, core: 2. Of those that a mesh axis runs over, the one named last changes fastest.
Arguments:
- queries: bfloat16 [8192, 2048], P('ctx', 'fsdp'), may hold values from -120 to 120
- keys: bfloat16 [8192, 256], P('ctx'), may hold values from -5 to 5
- values: bfloat16 [8192, 256], P('ctx'), may hold values from -5 to 5
- out_grad: bfloat16 [8192, 2048], P('ctx', 'fsdp'), may hold values from -5 to 5
- hidden: bfloat16 [8192, 8192], P('ctx', 'fsdp'), may hold values from -40 to 40
- key_weight: bfloat16 [8192, 256], P('fsdp'), may hold values from -10 to 10
- value_weight: bfloat16 [8192, 256], P('fsdp'), may hold values from -10 to 10
- stretch_owner: int32 [64], replicated, may hold values from 0 to 63, as said below
- positions: int32 [8192], P('ctx'), may hold values from 0 to 4095, as said below
Outputs:
- query_grad: bfloat16 [8192, 2048], P('ctx', 'fsdp')
- key_weight_grad: float32 [8192, 256], P('fsdp')
- value_weight_grad: float32 [8192, 256], P('fsdp')
Inputs may be any that keep to these rules, and one draw needn't show every extreme that they name: A permutation; index b of ctx holds sequence stretch stretch_owner[b] in its first 64 rows and stretch 2 * 64 - 1 - stretch_owner[b] in the others. `positions`: documents are contiguous in sequence order; a row's position counts from its document's first token, and the sequence's first token has position 0.
All inputs are finite; a program needn't handle non-finite values.
Results may differ from a plain program's by a relative error of at most 0.015.
Values may be sent and summed in bfloat16 or wider, within the bound.
A program may use at most 64 MiB of HBM per device.

v0:
```python
import math

import jax
import jax.numpy as jnp
from jax import lax
from jax.sharding import PartitionSpec as P

DH = 128
HPG = 8
KVG = 2


CLIP_RATE = 0.02
EPSILON = 1e-06
NEGATIVE = -1e30


def rows_by_head(block, heads, width):
    count = block.shape[0]
    return block.reshape(count, heads, width).transpose(1, 0, 2).reshape(heads * count, width)


def local(
    queries, keys, values, out_grad, hidden, key_weight, value_weight, stretch_owner, positions
):
    tok_dev = queries.shape[0]
    heads = queries.shape[1] // DH
    ctx_count = lax.axis_size("ctx")
    total = tok_dev * ctx_count
    half = tok_dev // 2
    ctx_index = lax.axis_index("ctx")
    group = lax.axis_index("fsdp") * heads // HPG
    scale = 1.0 / math.sqrt(DH)
    block = min(512, total)
    blocks = total // block
    query_count = heads * tok_dev
    own_keys = lax.dynamic_slice_in_dim(keys, group * DH, DH, 1)
    own_values = lax.dynamic_slice_in_dim(values, group * DH, DH, 1)
    all_keys, all_values = (
        lax.all_gather(own_keys, "ctx", axis=0, tiled=True),
        lax.all_gather(own_values, "ctx", axis=0, tiled=True),
    )
    offsets = jnp.arange(half, dtype=jnp.int32)
    stretches = jnp.stack([stretch_owner, 2 * ctx_count - 1 - stretch_owner], axis=1)
    key_place = (stretches[:, :, None] * half + offsets[None, None, :]).reshape(total)
    mine = lax.dynamic_slice_in_dim(stretches, ctx_index, 1, 0)[0]
    local_place = (mine[:, None] * half + offsets[None, :]).reshape(tok_dev)
    query_place = jnp.tile(local_place, heads)
    query_floor = jnp.tile(local_place - positions, heads)
    query_rows = rows_by_head(queries, heads, DH)
    grad_rows = rows_by_head(out_grad, heads, DH)
    contract_last = (((1,), (1,)), ((), ()))
    contract_first = (((0,), (0,)), ((), ()))

    def scores_at(start, width):
        key_block = lax.dynamic_slice_in_dim(all_keys, start, width, 0)
        place = lax.dynamic_slice_in_dim(key_place, start, width, 0)
        raw = (
            lax.dot_general(
                query_rows, key_block, contract_last, preferred_element_type=jnp.float32
            )
            * scale
        )
        seen = (place[None, :] <= query_place[:, None]) & (place[None, :] >= query_floor[:, None])
        return (jnp.where(seen, raw, NEGATIVE), seen, key_block)

    def stats_step(step, carry):
        top, mass = carry
        masked, seen, key_block = scores_at(step * block, block)
        new_top = jnp.maximum(top, jnp.max(masked, axis=1))
        weights = jnp.where(seen, jnp.exp(masked - new_top[:, None]), 0.0)
        mass = mass * jnp.exp(top - new_top) + jnp.sum(weights, axis=1)
        return (new_top, mass)

    start_top = jnp.full((query_count,), NEGATIVE, jnp.float32)
    start_mass = jnp.zeros((query_count,), jnp.float32)
    top, mass = lax.fori_loop(0, blocks, stats_step, (start_top, start_mass))
    lse = top + jnp.log(mass)

    def probs_at(start, width):
        masked, seen, key_block = scores_at(start, width)
        probs = jnp.where(seen, jnp.exp(masked - lse[:, None]), 0.0)
        value_block = lax.dynamic_slice_in_dim(all_values, start, width, 0)
        dprobs = lax.dot_general(
            grad_rows, value_block, contract_last, preferred_element_type=jnp.float32
        )
        return (probs, dprobs, key_block)

    def delta_step(step, acc):
        probs, dprobs, key_block = probs_at(step * block, block)
        return acc + jnp.sum(probs * dprobs, axis=1)

    delta = lax.fori_loop(0, blocks, delta_step, jnp.zeros((query_count,), jnp.float32))

    def slopes_at(start, width):
        probs, dprobs, key_block = probs_at(start, width)
        slopes = (probs * (dprobs - delta[:, None]) * scale).astype(jnp.bfloat16)
        return (probs.astype(jnp.bfloat16), slopes, key_block)

    def key_terms(probs_b, slopes):
        key_part = lax.dot_general(
            slopes, query_rows, contract_first, preferred_element_type=jnp.float32
        )
        value_part = lax.dot_general(
            probs_b, grad_rows, contract_first, preferred_element_type=jnp.float32
        )
        return jnp.concatenate([key_part, value_part], axis=1)

    start_query = jnp.zeros((query_count, DH), jnp.float32)

    def full_step(step, carry):
        query_acc, terms = carry
        start = step * block
        probs_b, slopes, key_block = slopes_at(start, block)
        query_acc = query_acc + jnp.dot(slopes, key_block, preferred_element_type=jnp.float32)
        terms = lax.dynamic_update_slice_in_dim(terms, key_terms(probs_b, slopes), start, 0)
        return (query_acc, terms)

    start_terms = jnp.zeros((total, 2 * DH), jnp.float32)
    query_acc, terms = lax.fori_loop(0, blocks, full_step, (start_query, start_terms))
    own_grads = lax.psum_scatter(terms, "ctx", scatter_dimension=0, tiled=True)
    query_grad = (
        query_acc.reshape(heads, tok_dev, DH)
        .transpose(1, 0, 2)
        .reshape(tok_dev, heads * DH)
        .astype(jnp.bfloat16)
    )
    members = lax.all_gather(own_grads.astype(jnp.bfloat16), "fsdp", axis=0, tiled=True).astype(
        own_grads.dtype
    )
    per_group = members.reshape(KVG, -1, tok_dev, 2 * DH).sum(axis=1)
    key_grads = (
        per_group[:, :, :DH].transpose(1, 0, 2).reshape(tok_dev, KVG * DH).astype(jnp.bfloat16)
    )
    value_grads = (
        per_group[:, :, DH:].transpose(1, 0, 2).reshape(tok_dev, KVG * DH).astype(jnp.bfloat16)
    )
    both_grads = jnp.concatenate([key_grads, value_grads], axis=1)
    columns = KVG * DH
    raw = lax.psum(
        lax.dot_general(hidden, both_grads, contract_first, preferred_element_type=jnp.float32),
        "ctx",
    )
    key_f = key_weight.astype(jnp.float32)
    value_f = value_weight.astype(jnp.float32)
    grad_sq, key_sq, value_sq = lax.psum(
        (
            jnp.sum(raw * raw, axis=0),
            jnp.sum(key_f * key_f, axis=0),
            jnp.sum(value_f * value_f, axis=0),
        ),
        "fsdp",
    )
    weight_norm = jnp.sqrt(jnp.concatenate([key_sq, value_sq]) + EPSILON)
    grad_norm = jnp.sqrt(grad_sq + EPSILON)
    clipped = raw * jnp.minimum(1.0, CLIP_RATE * total * weight_norm / grad_norm)[None, :]
    return (query_grad, clipped[:, :columns], clipped[:, columns:])


def solution(mesh):
    return jax.shard_map(
        local,
        mesh=mesh,
        in_specs=(
            P("ctx", "fsdp"),
            P("ctx", None),
            P("ctx", None),
            P("ctx", "fsdp"),
            P("ctx", "fsdp"),
            P("fsdp", None),
            P("fsdp", None),
            P(),
            P("ctx"),
        ),
        out_specs=(P("ctx", "fsdp"), P("fsdp", None), P("fsdp", None)),
        check_vma=False,
    )
```

profile of v0, /device:TPU:1, one launch (start us, length us, event | category | flops | bytes accessed | tf_op | source)
XLA Modules:
  0.0 690.4 jit_solution(3216926837924583909)
XLA Ops:
  7.2 1.4 constant_dynamic-slice_fusion.1
  8.7 1.4 constant_dynamic-slice_fusion
  14.8 78.1 %all-gather.3.cloned.1.call-done = bf16[8192,128]{1,0:T(8,128)(2,1)} async-done(((bf16[128,128]{1,0:T(8,128)(2,1)}), bf16[8192,128]{1,0:T(8,128)(2,1)}) %all-gather.3.cloned.1.call-update) | async-done | bytes 2097168 | tf_op jit(solution)/shard_map/all_gather | solution.py:40
  92.8 28.2 %while.46 = (s32[]{:T(128)}, f32[512]{0:T(512)S(1)}, f32[512]{0:T(512)S(1)}, s32[8192]{0:T(1024)S(1)}, bf16[8192,128]{1,0:T(8,128)(2,1)}, /*index=5*/bf16[512,12...) while((s32[]{:T(128)}, f32[512]{0:T(512)S(1)}, ...), condition=%wide.region_3.4_spmd.clone, body=%wide.region_0.3_spmd.clone.sunk | while | flops 70257160 | bytes 2407614 | solution.py:77
  121.1 50.1 %all-gather.5.cloned.1.call-done = bf16[8192,128]{1,0:T(8,128)(2,1)} async-done(((bf16[128,128]{1,0:T(8,128)(2,1)}), bf16[8192,128]{1,0:T(8,128)(2,1)}) %all-gather.5.cloned.1.call-update) | async-done | bytes 2097168 | tf_op jit(solution)/shard_map/all_gather | solution.py:41
  171.2 43.4 %while.47 = (s32[]{:T(128)}, f32[512]{0:T(512)S(1)}, s32[8192]{0:T(1024)S(1)}, bf16[8192,128]{1,0:T(8,128)(2,1)}, bf16[512,128]{1,0:T(8,128)(2,1)S(1)}, /*index=...) while((s32[]{:T(128)}, f32[512]{0:T(512)S(1)}, ...), condition=%wide.region_6.7_spmd.clone, body=%wide.region_4.6_spmd.clone.sunk | while | flops 136577536 | bytes 2647249 | solution.py:93
  176.7 1.4 fusion.98
  182.1 1.4 fusion.98
  187.5 1.4 fusion.98
  192.9 1.4 fusion.98
  198.3 1.4 fusion.98
  214.5 4.2 broadcast_in_dim.81
  218.7 86.9 %while.48 = (s32[]{:T(128)}, f32[512,128]{1,0:T(8,128)S(1)}, f32[8192,256]{0,1:T(8,128)}, s32[8192]{0:T(1024)S(1)}, bf16[8192,128]{1,0:T(8,128)(2,1)}, /*index=5...) while((s32[]{:T(128)}, f32[512,128]{1,0:T(8,128)S(1)}, ...), condition=%wide.region_8.9_spmd.clone, body=%wide.region_7.8_spmd.clone.sunk | while | flops 338952192 | bytes 7752937 | solution.py:120
  289.4 1.4 fusion.110
  305.7 145.3 %reduce-scatter.2.cloned.1.call-done = f32[128,256]{0,1:T(8,128)} async-done(((f32[8192,256]{0,1:T(8,128)}), f32[128,256]{0,1:T(8,128)}) %reduce-scatter.2.cloned.1.call-update) | async-done | bytes 131088 | tf_op jit(solution)/shard_map/reduce_scatter | solution.py:121
  451.9 9.1 %all_gather.11 = bf16[512,256]{0,1:T(8,128)(2,1)S(1)} all-gather(bf16[128,256]{0,1:T(8,128)(2,1)S(1)} %convert_element_type.54), channel_id=1, replica_groups=mesh['ctx'=64,'fsdp'=4] {'fsdp'}, dimensions={0}, use_global_device_ids=true | all-gather | bytes 327680 | tf_op jit(solution)/shard_map/all_gather | solution.py:128
  462.1 2.7 convolution_bitcast_fusion.1
  467.6 196.4 %all-reduce.3.cloned.1.call-done = f32[2048,512]{0,1:T(8,128)} async-done(((f32[2048,512]{0,1:T(8,128)}), f32[2048,512]{0,1:T(8,128)}) %all-reduce.3.cloned.1.call-update) | async-done | bytes 4194320 | tf_op jit(solution)/shard_map/psum | solution.py:140
  663.9 2.5 multiply_reduce_fusion
  666.5 8.5 %all-reduce = (f32[256]{0:T(256)S(1)}, f32[256]{0:T(256)S(1)}, f32[512]{0:T(512)S(1)}) all-reduce(f32[256]{0:T(256)S(1)} %get-tuple-element.720, f32[256]{0:T(256)S(1)} %get-tuple-element.721, f32[512]{0:T(512)S(1)} %multiply_reduce_fusion), channel_id=1, replica_groups=mesh['ctx'=64,'fsdp'=4] {'fsdp'}, use_global_device_ids=true, to_apply=%region_15.16 | all-reduce | flops 1024 | bytes 8192 | tf_op jit(solution)/shard_map/psum | solution.py:146
  674.9 2.5 broadcast_multiply_fusion
  677.5 1.7 fusion.54
  679.2 2.9 copy.33
  682.1 1.8 copy.34
  (355 shorter events, 157.4 us)
Async XLA Ops:
  7.2 454.9 %copy-start = (bf16[128,2048]{1,0:T(8,128)(2,1)S(1)}, bf16[128,2048]{1,0:T(8,128)(2,1)}, u32[]{:S(2)}) copy-start(bf16[128,2048]{1,0:T(8,128)(2,1)} %param.19) | copy-start | bytes 1572868
  7.2 85.7 %all-gather.3.cloned.1.call-start = ((), (), s32[]{:S(2)}) async-start(), calls=%async_computation.1 | async-start | bytes 2129920 | tf_op jit(solution)/shard_map/all_gather | solution.py:40
  8.7 162.5 %all-gather.5.cloned.1.call-start = ((), (), s32[]{:S(2)}) async-start(), calls=%async_computation.2 | async-start | bytes 2129920 | tf_op jit(solution)/shard_map/all_gather | solution.py:41
  10.1 440.9 %reduce-scatter.2.cloned.1.call-start = ((), (), s32[]{:S(2)}) async-start(), calls=%async_computation.3 | async-start | bytes 8519680 | tf_op jit(solution)/shard_map/reduce_scatter | solution.py:121
  305.6 358.3 %all-reduce.3.cloned.1.call-start = ((), (), s32[]{:S(2)}) async-start(), calls=%async_computation.4 | async-start | bytes 8388608 | tf_op jit(solution)/shard_map/psum | solution.py:140
  464.8 1.2 copy-start.1
  464.8 1.5 copy-start.2
Sparse Core Ops, SparseCore 0:
  11.3 81.4 all-gather.2
  96.2 74.9 all-gather.4
  305.8 145.2 reduce-scatter.1
  464.9 198.9 all-reduce.2
where the time goes:
time: 695 us; the launch traced here: 690 us
  waiting for transfers between devices  470 us (68%)
  matrix products  136 us (20%)
  other arithmetic  29 us (4%)
  local copies, waits for them, and re-layouts  21.9 us (3%)
  blocking collectives  17.6 us (3%)
  between operations  13.9 us (2%)
    psum x1, waiting for transfers between devices, local(): lax.psum(lax.dot_general(hidden, both_grads, contract_first, preferred_el...  196 us
    reduce_scatter x1, waiting for transfers between devices, local(): own_grads = lax.psum_scatter(terms, 'ctx', scatter_dimension=0, tiled=True)  145 us
    all_gather x1, waiting for transfers between devices, local(): lax.all_gather(own_keys, 'ctx', axis=0, tiled=True)  78.1 us
    dot_general x48, matrix products, scores_at(): lax.dot_general(query_rows, key_block, contract_last, preferred_element_t...  63.8 us
    all_gather x1, waiting for transfers between devices, local(): lax.all_gather(own_values, 'ctx', axis=0, tiled=True)  50.1 us
    dot_general x32, matrix products, probs_at(): lax.dot_general(grad_rows, value_block, contract_last, preferred_element_...  38.8 us
    dot_general x16, matrix products, full_step(): jnp.dot(slopes, key_block, preferred_element_type=jnp.float32)  20.5 us
  transfers between devices with their start and end apart: 4, of which 4 were waited for; matrix products, arithmetic and copies ran while one was open for 5% of the time, Pallas kernels for 0%

commit v1 on v0

v1 whole, which is shorter than its diff:
```python
import functools
import math

import jax
import jax.numpy as jnp
from jax import lax
from jax.experimental import pallas as pl
from jax.experimental.pallas import tpu as pltpu
from jax.sharding import PartitionSpec as P

DH = 128
HPG = 8
KVG = 2
TOK = 128
HALF = TOK // 2
Z = 8
X = 4
C = 2
Y = 4
G = X * C
PAIRS = Z * X * C
HEADS = 4
ROWS = G * TOK
CLIP_RATE = 0.02
EPSILON = 1e-06
NEGATIVE = -1e30
SCALE = 1.0 / math.sqrt(DH)
SCALE2 = SCALE * math.log2(math.e)
MESH = pl.DeviceIdType.MESH
ANY = pl.BlockSpec(memory_space=pl.ANY)
VMEM = pl.BlockSpec(memory_space=pltpu.VMEM)
SMEM = pl.BlockSpec(memory_space=pltpu.SMEM)
LAST = (((1,), (1,)), ((), ()))
FIRST = (((0,), (0,)), ((), ()))
BF16 = jnp.bfloat16
F32 = jnp.float32


class Place:
    def __init__(self):
        me = lax.axis_index("ctx")
        self.me = me
        self.y = lax.axis_index("fsdp")
        self.z = lax.div(me, G)
        self.slot = lax.rem(me, G)
        self.x = lax.div(self.slot, C)
        self.c = lax.rem(self.slot, C)

    def xslot(self, step, flip=False):
        x = lax.rem(self.x + step + X, X)
        return x * C + ((1 - self.c) if flip else self.c)

    def in_plane(self, slot):
        return {"ctx": self.z * G + slot}

    def zslot(self, step):
        return lax.rem(self.z + step + Z, Z)

    def in_column(self, z):
        return {"ctx": z * G + self.slot}

    def yslot(self, step):
        return lax.rem(self.y + step, Y)


class Copies:
    def __init__(self, send, recv):
        self.send, self.recv, self.made = send, recv, []

    def __call__(self, src, dst, device):
        i = len(self.made)
        copy = pltpu.make_async_remote_copy(
            src_ref=src,
            dst_ref=dst,
            send_sem=self.send.at[i],
            recv_sem=self.recv.at[i],
            device_id=device,
            device_id_type=MESH,
        )
        copy.start()
        self.made.append(copy)
        return copy

    def wait_sends(self):
        for copy in self.made:
            copy.wait_send()


def barrier(devices):
    sem = pltpu.get_barrier_semaphore()
    for device in devices:
        pl.semaphore_signal(sem, inc=1, device_id=device, device_id_type=MESH)
    pl.semaphore_wait(sem, len(devices))


def at(slot, rows, offset=0, count=None):
    return pl.ds(pl.multiple_of(slot * rows + offset, 16), rows if count is None else count)


def plane_ring(copies, p, src, out, rows):
    half = rows // 2
    right, left = p.xslot(1), p.xslot(-1)
    far = p.xslot(2)
    partner = p.in_plane(p.xslot(0, True))
    mine = out.at[at(p.slot, rows)]
    a = copies(src, mine, p.in_plane(right))
    b = copies(src, mine, p.in_plane(left))
    own = copies(src, mine, partner)
    yield
    a.wait_recv()
    first = out.at[at(left, rows, 0, half)]
    f = copies(first, first, p.in_plane(right))
    block = out.at[at(left, rows)]
    pa = copies(block, block, partner)
    b.wait_recv()
    second = out.at[at(right, rows, half, half)]
    g = copies(second, second, p.in_plane(left))
    block = out.at[at(right, rows)]
    pb = copies(block, block, partner)
    yield
    f.wait_recv()
    g.wait_recv()
    block = out.at[at(far, rows)]
    pc = copies(block, block, partner)
    yield
    own.wait_recv()
    pa.wait_recv()
    pb.wait_recv()
    pc.wait_recv()


def column_ring(copies, p, src, where):
    up, down = p.in_column(p.zslot(1)), p.in_column(p.zslot(-1))
    u = copies(src, where(p.z), up)
    d = copies(src, where(p.z), down)
    for step in range(1, Z // 2 + 1):
        yield
        u.wait_recv()
        if step < Z // 2:
            block = where(p.zslot(-step))
            u = copies(block, block, up)
        if step < Z // 2:
            d.wait_recv()
            if step < Z // 2 - 1:
                block = where(p.zslot(step))
                d = copies(block, block, down)


def run(*rings):
    rings = list(rings)
    while rings:
        rings = [ring for ring in rings if next(ring, True) is None]


def plane_peers(p):
    return [p.in_plane(p.xslot(s, f)) for s in range(X) for f in (False, True) if s or f]


def column_peers(p):
    return [p.in_column(p.zslot(s)) for s in range(1, Z)]


def row_peers(p):
    return [{"fsdp": p.yslot(s)} for s in range(1, Y)]


def gather_kernel(
    q, do, k, v, hid, pos, qg, dog, kg, vg, hg, pg, tq, tdo, tk, tv, th, tp, send, recv, local
):
    p = Place()
    group = lax.div(p.y * HEADS, HPG)
    cols = pl.ds(pl.multiple_of(group * DH, DH), DH)
    wide = hid.shape[1] // G
    own_hid = hid.at[:, pl.ds(pl.multiple_of(p.slot * wide, 128), wide)]
    own_k, own_v = k.at[:, cols], v.at[:, cols]
    mine = at(p.slot, TOK)
    moves = [
        (q, tq, qg.at[mine]),
        (do, tdo, dog.at[mine]),
        (own_k, tk, kg.at[at(p.z, TOK)]),
        (own_v, tv, vg.at[at(p.z, TOK)]),
        (own_hid, th, hg.at[mine]),
        (pos, tp, pg.at[p.slot]),
    ]
    loads = [pltpu.make_async_copy(s, t, local.at[i]) for i, (s, t, _) in enumerate(moves)]
    for load in loads:
        load.start()
    barrier(plane_peers(p) + [p.in_column(p.zslot(1)), p.in_column(p.zslot(-1))])
    copies = Copies(send, recv)
    rings = [
        column_ring(copies, p, own_k, lambda z: kg.at[at(z, TOK)]),
        plane_ring(copies, p, q, qg, TOK),
        column_ring(copies, p, own_v, lambda z: vg.at[at(z, TOK)]),
        plane_ring(copies, p, do, dog, TOK),
    ]
    for ring in rings:
        next(ring)
    stores = []
    for i, (_, t, d) in enumerate(moves):
        loads[i].wait()
        store = pltpu.make_async_copy(t, d, local.at[len(moves) + i])
        store.start()
        stores.append(store)
    small = []
    for s in range(X):
        for f in (False, True):
            if s or f:
                to = p.xslot(s, f)
                small.append(copies(pos, pg.at[p.slot], p.in_plane(to)))
    next(rings[0])
    next(rings[2])
    next(rings[1])
    next(rings[3])
    for s in range(X):
        for f in (False, True):
            if s or f:
                to = p.xslot(s, f)
                part = hid.at[:, pl.ds(pl.multiple_of(to * wide, 128), wide)]
                small.append(copies(part, hg.at[mine], p.in_plane(to)))
    run(*rings)
    for copy in small:
        copy.wait_recv()
    copies.wait_sends()
    for store in stores:
        store.wait()


def tile_bias(owners, pos, bias, j, p, width):
    lane = lax.broadcasted_iota(jnp.int32, (1, TOK), 1)
    low = lane < HALF
    places, floors = [], []
    for s in range(width // TOK):
        slot = j * (width // TOK) + s
        owner = owners[p.z * G + slot]
        place = lane + jnp.where(low, owner * HALF, (2 * PAIRS - 1 - owner) * HALF - HALF)
        places.append(place)
        floors.append(place - pos[slot, 0:1, :])
    place = jnp.concatenate(places, axis=1)
    floor = jnp.concatenate(floors, axis=1)
    row = lax.broadcasted_iota(jnp.int32, (HALF, width), 0)
    for z in range(Z):
        owner = owners[z * G + p.slot]
        for h, stretch in enumerate((owner, 2 * PAIRS - 1 - owner)):
            key = row + stretch * HALF
            seen = (key <= place) & (key >= floor)
            bias[pl.ds(z * TOK + h * HALF, HALF), :] = jnp.where(seen, 0.0, NEGATIVE)


def stats_kernel(owners, pos, q, do, k, v, out, bias):
    p = Place()
    width = q.shape[0]
    tile_bias(owners, pos, bias, pl.program_id(0), p, width)
    for h in range(HEADS):
        cols = pl.ds(h * DH, DH)
        raw = lax.dot_general(k[...], q[:, cols], LAST, preferred_element_type=F32) + bias[...]
        top = jnp.max(raw, axis=0, keepdims=True)
        mass = jnp.exp2((raw - top) * SCALE2)
        total = jnp.sum(mass, axis=0, keepdims=True)
        dp = lax.dot_general(v[...], do[:, cols], LAST, preferred_element_type=F32)
        dsum = jnp.sum(mass * dp, axis=0, keepdims=True)
        out[h : h + 1, :] = top * SCALE2 + jnp.log2(total)
        out[HEADS + h : HEADS + h + 1, :] = dsum / total


def share_kernel(stats, out, send, recv, local):
    p = Place()
    load = pltpu.make_async_copy(stats, out.at[p.slot], local.at[0])
    load.start()
    barrier(plane_peers(p))
    copies = Copies(send, recv)
    made = [copies(stats, out.at[p.slot], peer) for peer in plane_peers(p)]
    for copy in made:
        copy.wait_recv()
    copies.wait_sends()
    load.wait()


def grads_kernel(owners, pos, stats, q, do, k, v, dq, dkv, bias, kt, probs, slopes, acc):
    p = Place()
    j = pl.program_id(0)
    width = q.shape[0]

    @pl.when(j == 0)
    def _():
        kt[...] = k[...].T
        acc[...] = jnp.zeros_like(acc)

    tile_bias(owners, pos, bias, j, p, width)
    for h in range(HEADS):
        cols = pl.ds(h * DH, DH)
        parts = stats[:, h, :]
        top = jnp.max(parts, axis=0, keepdims=True)
        weight = jnp.exp2(parts - top)
        total = jnp.sum(weight, axis=0, keepdims=True)
        lse = top + jnp.log2(total)
        delta = jnp.sum(weight * stats[:, HEADS + h, :], axis=0, keepdims=True) / total
        raw = lax.dot_general(k[...], q[:, cols], LAST, preferred_element_type=F32) + bias[...]
        prob = jnp.exp2(raw * SCALE2 - lse)
        dp = lax.dot_general(v[...], do[:, cols], LAST, preferred_element_type=F32)
        slope = (prob * (dp - delta)).astype(BF16)
        at_h = pl.ds(h * width, width)
        probs[:, at_h] = prob.astype(BF16)
        slopes[:, at_h] = slope
        dqt = jnp.dot(kt[...], slopes[:, at_h], preferred_element_type=F32)
        dq[:, cols] = (dqt * SCALE).T.astype(BF16)
    tall = lambda ref: jnp.concatenate([ref[:, pl.ds(h * DH, DH)] for h in range(HEADS)], axis=0)
    acc[:, :DH] += jnp.dot(slopes[...], tall(q), preferred_element_type=F32)
    acc[:, DH:] += jnp.dot(probs[...], tall(do), preferred_element_type=F32)

    @pl.when(j == pl.num_programs(0) - 1)
    def _():
        dkv[:, :DH] = (acc[:, :DH] * SCALE).astype(BF16)
        dkv[:, DH:] = acc[:, DH:].astype(BF16)


def reduce_kernel(dq, dkv, dq_slots, grads, tq, gz, ysend, gy, both, send, recv, local):
    p = Place()
    own_q = pltpu.make_async_copy(dq.at[at(p.slot, TOK)], tq, local.at[0])
    own_q.start()
    own_g = pltpu.make_async_copy(dkv.at[at(p.z, TOK)], gz.at[p.z], local.at[1])
    own_g.start()
    barrier(
        plane_peers(p) + column_peers(p) + row_peers(p)
    )
    copies = Copies(send, recv)
    zs = [
        copies(dkv.at[at(p.zslot(s), TOK)], gz.at[p.z], p.in_column(p.zslot(s)))
        for s in (4, 3, 5, 2, 6, 1, 7)
    ]
    qs = []
    for s, f in ((2, False), (2, True), (1, False), (3, False), (1, True), (3, True), (0, True)):
        to = p.xslot(s, f)
        qs.append(copies(dq.at[at(to, TOK)], dq_slots.at[p.slot], p.in_plane(to)))
    own_q.wait()
    put_q = pltpu.make_async_copy(tq, dq_slots.at[p.slot], local.at[2])
    put_q.start()
    own_g.wait()
    for copy in zs:
        copy.wait_recv()
    total = gz[0].astype(F32)
    for z in range(1, Z):
        total = total + gz[z].astype(F32)
    ysend[...] = total.astype(BF16)
    gy[p.y] = total.astype(BF16)
    ys = [copies(ysend, gy.at[p.y], peer) for peer in row_peers(p)]
    for copy in ys:
        copy.wait_recv()
    members = Y // KVG
    for g in range(KVG):
        part = gy[g * members].astype(F32)
        for i in range(1, members):
            part = part + gy[g * members + i].astype(F32)
        both[:, g * DH : (g + 1) * DH] = part[:, :DH].astype(BF16)
        both[:, (KVG + g) * DH : (KVG + g + 1) * DH] = part[:, DH:].astype(BF16)
    put_g = pltpu.make_async_copy(both, grads.at[at(p.slot, TOK)], local.at[3])
    put_g.start()
    run(plane_ring(copies, p, both, grads, TOK))
    for copy in qs:
        copy.wait_recv()
    copies.wait_sends()
    put_q.wait()
    put_g.wait()


def finish_kernel(part, weights, raw, sums, rz, buf, send, recv, local):
    p = Place()
    rows = part.shape[0]
    piece = rows // Z
    own = pltpu.make_async_copy(part.at[at(p.z, piece)], rz.at[p.z], local.at[0])
    own.start()
    barrier(plane_peers(p) + column_peers(p) + row_peers(p))
    copies = Copies(send, recv)
    zs = [
        copies(part.at[at(p.zslot(s), piece)], rz.at[p.z], p.in_column(p.zslot(s)))
        for s in (4, 3, 5, 2, 6, 1, 7)
    ]
    own.wait()
    for copy in zs:
        copy.wait_recv()
    total = rz[0].astype(F32)
    for z in range(1, Z):
        total = total + rz[z].astype(F32)
    where = lambda z: buf.at[pl.ds(pl.multiple_of(p.slot * rows + z * piece, 16), piece)]
    mine = pl.ds(pl.multiple_of(p.slot * rows + p.z * piece, 16), piece)
    buf[mine, :] = total.astype(BF16)
    run(column_ring(copies, p, where(p.z), where))
    run(plane_ring(copies, p, buf.at[at(p.slot, rows)], buf, rows))
    put = pltpu.make_async_copy(buf, raw, local.at[1])
    put.start()
    width = buf.shape[1]

    def step(i, acc):
        block = buf[pl.ds(pl.multiple_of(i * 64, 64), 64), :].astype(F32)
        return acc + jnp.sum((block * block).reshape(8, 8, width), axis=0)

    acc = lax.fori_loop(0, buf.shape[0] // 64, step, jnp.zeros((8, width), F32))
    row = lax.broadcasted_iota(jnp.int32, (8, width), 0)
    sums[p.y] = jnp.where(row == 0, jnp.sum(acc, axis=0, keepdims=True), weights[...])
    ys = [copies(sums.at[p.y], sums.at[p.y], peer) for peer in row_peers(p)]
    for copy in ys:
        copy.wait_recv()
    copies.wait_sends()
    put.wait()


def remote(ident, kernel, **kw):
    return pl.pallas_call(
        kernel,
        compiler_params=pltpu.CompilerParams(
            collective_id=ident, has_side_effects=True, vmem_limit_bytes=40 * 1024 * 1024
        ),
        **kw,
    )


def shape(dims, kind=BF16):
    return jax.ShapeDtypeStruct(dims, kind)


def dma(n):
    return pltpu.SemaphoreType.DMA((n,))


def local(
    queries, keys, values, out_grad, hidden, key_weight, value_weight, stretch_owner, positions
):
    width = queries.shape[1]
    model = hidden.shape[1]
    piece = model // G
    columns = KVG * DH
    pos = jnp.broadcast_to(positions[None, :], (8, TOK))
    qg, dog, kg, vg, hg, pg = remote(
        0,
        gather_kernel,
        out_shape=(
            shape((ROWS, width)),
            shape((ROWS, width)),
            shape((Z * TOK, DH)),
            shape((Z * TOK, DH)),
            shape((ROWS, piece)),
            shape((G, 8, TOK), jnp.int32),
        ),
        in_specs=[ANY] * 6,
        out_specs=(ANY,) * 6,
        scratch_shapes=[
            pltpu.VMEM((TOK, width), BF16),
            pltpu.VMEM((TOK, width), BF16),
            pltpu.VMEM((TOK, DH), BF16),
            pltpu.VMEM((TOK, DH), BF16),
            pltpu.VMEM((TOK, piece), BF16),
            pltpu.VMEM((8, TOK), jnp.int32),
            dma(64),
            dma(64),
            dma(12),
        ],
    )(queries, out_grad, keys, values, hidden, pos)
    tile = 256
    q_spec = pl.BlockSpec((tile, width), lambda j: (j, 0))
    k_spec = pl.BlockSpec((Z * TOK, DH), lambda j: (0, 0))
    pos_spec = pl.BlockSpec((G, 8, TOK), lambda j: (0, 0, 0))
    params = pltpu.CompilerParams(
        dimension_semantics=("arbitrary",), vmem_limit_bytes=48 * 1024 * 1024
    )
    stats = pl.pallas_call(
        stats_kernel,
        grid=(ROWS // tile,),
        out_shape=shape((2 * HEADS, ROWS), F32),
        in_specs=[SMEM, pos_spec, q_spec, q_spec, k_spec, k_spec],
        out_specs=pl.BlockSpec((2 * HEADS, tile), lambda j: (0, j)),
        scratch_shapes=[pltpu.VMEM((Z * TOK, tile), F32)],
        compiler_params=params,
    )(stretch_owner, pg, qg, dog, kg, vg)
    shared = remote(
        1,
        share_kernel,
        out_shape=shape((G, 2 * HEADS, ROWS), F32),
        in_specs=[VMEM],
        out_specs=VMEM,
        scratch_shapes=[dma(8), dma(8), dma(1)],
    )(stats)
    dq, dkv = pl.pallas_call(
        grads_kernel,
        grid=(ROWS // tile,),
        out_shape=(shape((ROWS, width)), shape((Z * TOK, 2 * DH))),
        in_specs=[
            SMEM,
            pos_spec,
            pl.BlockSpec((G, 2 * HEADS, tile), lambda j: (0, 0, j)),
            q_spec,
            q_spec,
            k_spec,
            k_spec,
        ],
        out_specs=(q_spec, pl.BlockSpec((Z * TOK, 2 * DH), lambda j: (0, 0))),
        scratch_shapes=[
            pltpu.VMEM((Z * TOK, tile), F32),
            pltpu.VMEM((DH, Z * TOK), BF16),
            pltpu.VMEM((Z * TOK, HEADS * tile), BF16),
            pltpu.VMEM((Z * TOK, HEADS * tile), BF16),
            pltpu.VMEM((Z * TOK, 2 * DH), F32),
        ],
        compiler_params=params,
    )(stretch_owner, pg, shared, qg, dog, kg, vg)
    dq_slots, grads = remote(
        2,
        reduce_kernel,
        out_shape=(shape((G, TOK, width)), shape((ROWS, 2 * columns))),
        in_specs=[ANY, ANY],
        out_specs=(ANY, ANY),
        scratch_shapes=[
            pltpu.VMEM((TOK, width), BF16),
            pltpu.VMEM((Z, TOK, 2 * DH), BF16),
            pltpu.VMEM((TOK, 2 * DH), BF16),
            pltpu.VMEM((Y, TOK, 2 * DH), BF16),
            pltpu.VMEM((TOK, 2 * columns), BF16),
            dma(40),
            dma(40),
            dma(4),
        ],
    )(dq, dkv)
    query_grad = jnp.sum(dq_slots.astype(F32), axis=0).astype(BF16)
    part = lax.dot_general(hg, grads, FIRST, preferred_element_type=F32).astype(BF16)
    key_f = key_weight.astype(F32)
    value_f = value_weight.astype(F32)
    weight_sq = jnp.concatenate([jnp.sum(key_f * key_f, axis=0), jnp.sum(value_f * value_f, axis=0)])
    raw, sums = remote(
        3,
        finish_kernel,
        out_shape=(shape((model, 2 * columns)), shape((Y, 8, 2 * columns), F32)),
        in_specs=[ANY, VMEM],
        out_specs=(ANY, VMEM),
        scratch_shapes=[
            pltpu.VMEM((Z, piece // Z, 2 * columns), BF16),
            pltpu.VMEM((model, 2 * columns), BF16),
            dma(40),
            dma(40),
            dma(2),
        ],
    )(part, jnp.broadcast_to(weight_sq[None, :], (8, 2 * columns)))
    total = jnp.sum(sums, axis=0)
    grad_norm = jnp.sqrt(total[0] + EPSILON)
    weight_norm = jnp.sqrt(total[1] + EPSILON)
    tokens = TOK * PAIRS
    factor = jnp.minimum(1.0, CLIP_RATE * tokens * weight_norm / grad_norm)
    key_out = raw[:, :columns].astype(F32) * factor[None, :columns]
    value_out = raw[:, columns:].astype(F32) * factor[None, columns:]
    return (query_grad, key_out, value_out)


def solution(mesh):
    return jax.shard_map(
        local,
        mesh=mesh,
        in_specs=(
            P("ctx", "fsdp"),
            P("ctx", None),
            P("ctx", None),
            P("ctx", "fsdp"),
            P("ctx", "fsdp"),
            P("fsdp", None),
            P("fsdp", None),
            P(),
            P("ctx"),
        ),
        out_specs=(P("ctx", "fsdp"), P("fsdp", None), P("fsdp", None)),
        check_vma=False,
    )
```

time: 695 us -> 137 us (0.20)
  waiting for transfers between devices: 470 us -> 0 us
  matrix products: 136 us -> 0.45 us
  Pallas kernels: 0 us -> 131 us
  other arithmetic: 29 us -> 5.22 us
  local copies, waits for them, and re-layouts: 21.9 us -> 0.04 us
  blocking collectives: 17.6 us -> 0 us
  between operations: 13.9 us -> 0.84 us
    psum x1 -> x0, waiting for transfers between devices: 196 us -> none  [local(): lax.psum(lax.dot_general(hidden, both_grads, contract_first, preferred_el...]
    reduce_scatter x1 -> x0, waiting for transfers between devices: 145 us -> none  [local(): own_grads = lax.psum_scatter(terms, 'ctx', scatter_dimension=0, tiled=True)]
    dot_general x129 -> x1, matrix products: 136 us -> 0.45 us  [local(): lax.dot_general(hg, grads, FIRST, preferred_element_type=F32).astype(BF16)]
    pallas_call x0 -> x6, Pallas kernels: none -> 131 us  [the longest x1 39.4 us: local(): remote(3, finish_kernel, out_shape=(shape((model, 2 * columns)), shape((Y...]
    all_gather x2 -> x0, waiting for transfers between devices: 128 us -> none  [the longest x1 78.1 us: local(): lax.all_gather(own_keys, 'ctx', axis=0, tiled=True)]
    dynamic_update_slice x16 -> x0, other arithmetic: 13.7 us -> none  [full_step(): lax.dynamic_update_slice_in_dim(terms, key_terms(probs_b, slopes), start, 0)]
    all_gather x1 -> x0, blocking collectives: 9.14 us -> none  [local(): lax.all_gather(own_grads.astype(jnp.bfloat16), 'fsdp', axis=0, tiled=True)]
    psum x1 -> x0, blocking collectives: 8.46 us -> none  [local(): lax.psum((jnp.sum(raw * raw, axis=0), jnp.sum(key_f * key_f, axis=0), jnp...]
  transfers between devices with their start and end apart: 4 -> 0, of which waited for: 4 -> 0; matrix products, arithmetic and copies ran while one was open for 5% -> 0% of each run, Pallas kernels for 0% -> 0%
where the time goes in v1:
time: 137 us
  Pallas kernels  131 us (96%)
  other arithmetic  5.22 us (4%)
    pallas_call x1, Pallas kernels, local(): remote(3, finish_kernel, out_shape=(shape((model, 2 * columns)), shape((Y...  39.4 us
    pallas_call x1, Pallas kernels, local(): remote(2, reduce_kernel, out_shape=(shape((G, TOK, width)), shape((ROWS,...  33.9 us
    pallas_call x1, Pallas kernels, local(): remote(0, gather_kernel, out_shape=(shape((ROWS, width)), shape((ROWS, wi...  26.4 us
    pallas_call x1, Pallas kernels, local(): pl.pallas_call(grads_kernel, grid=(ROWS // tile,), out_shape=(shape((ROWS...  13.4 us
    pallas_call x1, Pallas kernels, local(): remote(1, share_kernel, out_shape=shape((G, 2 * HEADS, ROWS), F32), in_sp...  8.86 us
    pallas_call x1, Pallas kernels, local(): pl.pallas_call(stats_kernel, grid=(ROWS // tile,), out_shape=shape((2 * H...  8.54 us

profile of v1, /device:TPU:1, one launch (start us, length us, event | category | flops | bytes accessed | tf_op | source)
XLA Modules:
  0.0 137.1 jit_solution(944202017392910133)
XLA Ops:
  0.6 0.0 copy-start.5
  0.6 0.0 copy-start.6
  0.7 0.0 copy-start
  0.7 0.0 copy-start.2
  0.7 0.0 copy-start.4
  0.7 0.0 copy-start.3
  0.7 0.0 copy-start.1
  0.7 2.1 %multiply_reduce_fusion = (f32[256]{0:T(256)S(1)}, f32[256]{0:T(256)S(1)}) fusion(bf16[2048,256]{1,0:T(8,128)(2,1)} %param.15, bf16[2048,256]{1,0:T(8,128)(2,1)} %param.14), kind=kLoop, calls=%fused_computation.2 | loop fusion | flops 3145216 | bytes 2099200 | tf_op jit(solution)/shard_map/reduce_sum | solution.py:525
  2.8 0.0 copy-done.6
  2.8 0.0 copy-done
  2.8 0.0 copy-done.2
  2.8 0.0 copy-done.4
  2.9 0.0 copy-done.3
  2.9 0.0 copy-done.1
  2.9 26.4 %shard_map.112 = (bf16[1024,512]{1,0:T(8,128)(2,1)S(1)}, bf16[1024,512]{1,0:T(8,128)(2,1)S(1)}, bf16[1024,128]{1,0:T(8,128)(2,1)S(1)}, bf16[1024,128]{1,0:T(8,12...) custom-call(bf16[128,512]{1,0:T(8,128)(2,1)S(1)} %copy-done.1, bf16[128,512]{1,0:T(8,128)(2,1)S(1)} %copy-done.2, ...), custom_call_target="tpu_custom_call" | custom-call | tf_op jit(solution)/shard_map/pallas_call | solution.py:432
  29.3 0.0 copy-done.5
  29.3 8.5 %shard_map.113.stats = f32[8,1024]{1,0:T(8,128)S(1)} custom-call(s32[64]{0:T(128)S(1)} %copy-done.5, s32[8,8,128]{2,1,0:T(8,128)S(1)} %get-tuple-element.15.pos, bf16[1024,512]{1,0:T(8,128)(2,1)S(1)} %get-tuple-element.16.q, bf16[1024,512]{1,0:T(8,128)(2,1)S(1)} %get-tuple-element.17.do, bf16[1024,128]{1,0:T(8,128)(2,1)S(1)} %get-tuple-element.18.k, ...), custom_call_target="tpu_custom_call" | custom-call | tf_op jit(solution)/shard_map/pallas_call | solution.py:464
  37.9 8.9 %shard_map.114.stats = f32[8,8,1024]{2,1,0:T(8,128)S(1)} custom-call(f32[8,1024]{1,0:T(8,128)S(1)} %shard_map.113.stats), custom_call_target="tpu_custom_call" | custom-call | tf_op jit(solution)/shard_map/pallas_call | solution.py:473
  46.7 13.4 %shard_map.115 = (bf16[1024,512]{1,0:T(8,128)(2,1)S(1)}, bf16[1024,256]{1,0:T(8,128)(2,1)S(1)}) custom-call(s32[64]{0:T(128)S(1)} %copy-done.5, s32[8,8,128]{2,1,0:T(8,128)S(1)} %get-tuple-element.15.pos, f32[8,8,1024]{2,1,0:T(8,128)S(1)} %shard_map.114.stats, bf16[1024,512]{1,0:T(8,128)(2,1)S(1)} %get-tuple-element.16.q, ...), custom_call_target="tpu_custom_call" | custom-call | tf_op jit(solution)/shard_map/pallas_call | solution.py:481
  60.1 33.9 %shard_map.116 = (bf16[8,128,512]{2,1,0:T(8,128)(2,1)S(1)}, bf16[1024,512]{1,0:T(8,128)(2,1)S(1)}) custom-call(bf16[1024,512]{1,0:T(8,128)(2,1)S(1)} %get-tuple-element.20.dq, bf16[1024,256]{1,0:T(8,128)(2,1)S(1)} %get-tuple-element.21.dkv), custom_call_target="tpu_custom_call" | custom-call | tf_op jit(solution)/shard_map/pallas_call | solution.py:504
  94.1 0.5 convolution_convert_fusion.part
  94.5 0.8 reduce_sum.39
  95.3 39.4 %shard_map.117 = (bf16[2048,512]{1,0:T(8,128)(2,1)S(1)}, f32[4,8,512]{2,1,0:T(8,128)S(1)}) custom-call(bf16[256,512]{1,0:T(8,128)(2,1)S(1)} %convolution_convert_fusion.part, f32[8,512]{1,0:T(8,128)S(1)} %broadcast_in_dim.5.weights), custom_call_target="tpu_custom_call" | custom-call | tf_op jit(solution)/shard_map/pallas_call | solution.py:526
  134.8 2.3 %convert_multiply_fusion = (f32[2048,256]{1,0:T(8,128)}, f32[2048,256]{1,0:T(8,128)}) fusion(f32[256]{0:T(256)S(1)} %bitcast.4, bf16[2048,512]{1,0:T(8,128)(2,1)S(1)} %get-tuple-element.25, f32[256]{0:T(256)S(1)} %bitcast.5), kind=kLoop, calls=%fused_computation | loop fusion | flops 2097152 | bytes 6293504 | tf_op jit(solution)/shard_map/mul | solution.py:546
  (6 shorter events, 0.0 us)
Async XLA Ops:
  0.6 28.7 %copy-start.5 = (s32[64]{0:T(128)S(1)}, s32[64]{0:T(128)}, u32[]{:S(2)}) copy-start(s32[64]{0:T(128)} %owners.3) | copy-start | bytes 772
  0.6 2.2 %copy-start.6 = (s32[128]{0:T(128)S(1)}, s32[128]{0:T(128)}, u32[]{:S(2)}) copy-start(s32[128]{0:T(128)} %param.17) | copy-start | bytes 1540
  0.7 2.2 %copy-start = (bf16[128,2048]{1,0:T(8,128)(2,1)S(1)}, bf16[128,2048]{1,0:T(8,128)(2,1)}, u32[]{:S(2)}) copy-start(bf16[128,2048]{1,0:T(8,128)(2,1)} %hid.1) | copy-start | bytes 1572868
  0.7 2.2 %copy-start.2 = (bf16[128,512]{1,0:T(8,128)(2,1)S(1)}, bf16[128,512]{1,0:T(8,128)(2,1)}, u32[]{:S(2)}) copy-start(bf16[128,512]{1,0:T(8,128)(2,1)} %do.1) | copy-start | bytes 393220
  0.7 2.2 %copy-start.4 = (bf16[128,256]{1,0:T(8,128)(2,1)S(1)}, bf16[128,256]{1,0:T(8,128)(2,1)}, u32[]{:S(2)}) copy-start(bf16[128,256]{1,0:T(8,128)(2,1)} %v.1) | copy-start | bytes 196612
  0.7 2.2 %copy-start.3 = (bf16[128,256]{1,0:T(8,128)(2,1)S(1)}, bf16[128,256]{1,0:T(8,128)(2,1)}, u32[]{:S(2)}) copy-start(bf16[128,256]{1,0:T(8,128)(2,1)} %k.1) | copy-start | bytes 196612
  0.7 2.2 %copy-start.1 = (bf16[128,512]{1,0:T(8,128)(2,1)S(1)}, bf16[128,512]{1,0:T(8,128)(2,1)}, u32[]{:S(2)}) copy-start(bf16[128,512]{1,0:T(8,128)(2,1)} %q.1) | copy-start | bytes 393220

commit v2 on v1

--- a/solution.py
+++ b/solution.py
@@ -97,36 +97,40 @@
     return pl.ds(pl.multiple_of(slot * rows + offset, 16), rows if count is None else count)
 
 
-def plane_ring(copies, p, src, out, rows):
+def plane_ring(copies, p, src, where, rows):
     half = rows // 2
     right, left = p.xslot(1), p.xslot(-1)
     far = p.xslot(2)
     partner = p.in_plane(p.xslot(0, True))
-    mine = out.at[at(p.slot, rows)]
+    mine = where(p.slot, 0, rows)
     a = copies(src, mine, p.in_plane(right))
     b = copies(src, mine, p.in_plane(left))
     own = copies(src, mine, partner)
     yield
     a.wait_recv()
-    first = out.at[at(left, rows, 0, half)]
+    first = where(left, 0, half)
     f = copies(first, first, p.in_plane(right))
-    block = out.at[at(left, rows)]
+    block = where(left, 0, rows)
     pa = copies(block, block, partner)
     b.wait_recv()
-    second = out.at[at(right, rows, half, half)]
+    second = where(right, half, half)
     g = copies(second, second, p.in_plane(left))
-    block = out.at[at(right, rows)]
+    block = where(right, 0, rows)
     pb = copies(block, block, partner)
     yield
     f.wait_recv()
     g.wait_recv()
-    block = out.at[at(far, rows)]
+    block = where(far, 0, rows)
     pc = copies(block, block, partner)
     yield
     own.wait_recv()
     pa.wait_recv()
     pb.wait_recv()
     pc.wait_recv()
+
+
+def whole(ref, rows):
+    return lambda slot, offset, count: ref.at[at(slot, rows, offset, count)]
 
 
 def column_ring(copies, p, src, where):
@@ -164,14 +168,23 @@
     return [{"fsdp": p.yslot(s)} for s in range(1, Y)]
 
 
+def sum_squares(ref, chunk=64):
+    width = ref.shape[1]
+
+    def step(i, acc):
+        block = ref[pl.ds(pl.multiple_of(i * chunk, chunk), chunk), :].astype(F32)
+        return acc + jnp.sum((block * block).reshape(chunk // 8, 8, width), axis=0)
+
+    acc = lax.fori_loop(0, ref.shape[0] // chunk, step, jnp.zeros((8, width), F32))
+    return jnp.sum(acc, axis=0, keepdims=True)
+
+
 def gather_kernel(
-    q, do, k, v, hid, pos, qg, dog, kg, vg, hg, pg, tq, tdo, tk, tv, th, tp, send, recv, local
+    q, do, k, v, pos, kw, vw, qg, dog, kg, vg, pg, wsum, tq, tdo, tk, tv, tp, tkw, tvw, send, recv, local
 ):
     p = Place()
     group = lax.div(p.y * HEADS, HPG)
     cols = pl.ds(pl.multiple_of(group * DH, DH), DH)
-    wide = hid.shape[1] // G
-    own_hid = hid.at[:, pl.ds(pl.multiple_of(p.slot * wide, 128), wide)]
     own_k, own_v = k.at[:, cols], v.at[:, cols]
     mine = at(p.slot, TOK)
     moves = [
@@ -179,19 +192,24 @@
         (do, tdo, dog.at[mine]),
         (own_k, tk, kg.at[at(p.z, TOK)]),
         (own_v, tv, vg.at[at(p.z, TOK)]),
-        (own_hid, th, hg.at[mine]),
         (pos, tp, pg.at[p.slot]),
     ]
     loads = [pltpu.make_async_copy(s, t, local.at[i]) for i, (s, t, _) in enumerate(moves)]
     for load in loads:
         load.start()
+    heavy = [
+        pltpu.make_async_copy(s, t, local.at[2 * len(moves) + i])
+        for i, (s, t) in enumerate(((kw, tkw), (vw, tvw)))
+    ]
+    for load in heavy:
+        load.start()
     barrier(plane_peers(p) + [p.in_column(p.zslot(1)), p.in_column(p.zslot(-1))])
     copies = Copies(send, recv)
     rings = [
         column_ring(copies, p, own_k, lambda z: kg.at[at(z, TOK)]),
-        plane_ring(copies, p, q, qg, TOK),
+        plane_ring(copies, p, q, whole(qg, TOK), TOK),
         column_ring(copies, p, own_v, lambda z: vg.at[at(z, TOK)]),
-        plane_ring(copies, p, do, dog, TOK),
+        plane_ring(copies, p, do, whole(dog, TOK), TOK),
     ]
     for ring in rings:
         next(ring)
@@ -201,22 +219,12 @@
         store = pltpu.make_async_copy(t, d, local.at[len(moves) + i])
         store.start()
         stores.append(store)
-    small = []
-    for s in range(X):
-        for f in (False, True):
-            if s or f:
-                to = p.xslot(s, f)
-                small.append(copies(pos, pg.at[p.slot], p.in_plane(to)))
-    next(rings[0])
-    next(rings[2])
-    next(rings[1])
-    next(rings[3])
-    for s in range(X):
-        for f in (False, True):
-            if s or f:
-                to = p.xslot(s, f)
-                part = hid.at[:, pl.ds(pl.multiple_of(to * wide, 128), wide)]
-                small.append(copies(part, hg.at[mine], p.in_plane(to)))
+    small = [copies(pos, pg.at[p.slot], peer) for peer in plane_peers(p)]
+    for load in heavy:
+        load.wait()
+    wsum[...] = jnp.broadcast_to(
+        jnp.concatenate([sum_squares(tkw), sum_squares(tvw)], axis=1), wsum.shape
+    )
     run(*rings)
     for copy in small:
         copy.wait_recv()
@@ -313,26 +321,50 @@
         dkv[:, DH:] = acc[:, DH:].astype(BF16)
 
 
-def reduce_kernel(dq, dkv, dq_slots, grads, tq, gz, ysend, gy, both, send, recv, local):
+def reduce_kernel(
+    dq, dkv, hid, dq_slots, grads, hg, th, dqa, pq, cq, gz, ysend, gy, both, send, recv, local
+):
     p = Place()
-    own_q = pltpu.make_async_copy(dq.at[at(p.slot, TOK)], tq, local.at[0])
-    own_q.start()
+    wide = hid.shape[1] // G
+    mine = at(p.slot, TOK)
+
+    def strip(slot):
+        return hid.at[:, pl.ds(pl.multiple_of(slot * wide, 128), wide)]
+
+    own_h = pltpu.make_async_copy(strip(p.slot), th, local.at[0])
+    own_h.start()
     own_g = pltpu.make_async_copy(dkv.at[at(p.z, TOK)], gz.at[p.z], local.at[1])
     own_g.start()
-    barrier(
-        plane_peers(p) + column_peers(p) + row_peers(p)
-    )
+    kept = [
+        pltpu.make_async_copy(dq.at[at(x * C + p.c, TOK)], dqa.at[x], local.at[5 + x])
+        for x in range(X)
+    ]
+    for load in kept:
+        load.start()
+    barrier(plane_peers(p) + column_peers(p) + row_peers(p))
     copies = Copies(send, recv)
     zs = [
         copies(dkv.at[at(p.zslot(s), TOK)], gz.at[p.z], p.in_column(p.zslot(s)))
         for s in (4, 3, 5, 2, 6, 1, 7)
     ]
-    qs = []
+    partner = p.in_plane(p.xslot(0, True))
+    given = [copies(dq.at[at(x * C + 1 - p.c, TOK)], pq.at[x], partner) for x in range(X)]
+    hs = []
     for s, f in ((2, False), (2, True), (1, False), (3, False), (1, True), (3, True), (0, True)):
         to = p.xslot(s, f)
-        qs.append(copies(dq.at[at(to, TOK)], dq_slots.at[p.slot], p.in_plane(to)))
-    own_q.wait()
-    put_q = pltpu.make_async_copy(tq, dq_slots.at[p.slot], local.at[2])
+        hs.append(copies(strip(to), hg.at[mine], p.in_plane(to)))
+    own_h.wait()
+    put_h = pltpu.make_async_copy(th, hg.at[mine], local.at[2])
+    put_h.start()
+    for x in range(X):
+        kept[x].wait()
+        given[x].wait_recv()
+        cq[x] = (dqa[x].astype(F32) + pq[x].astype(F32)).astype(BF16)
+    qs = []
+    for s in (2, 1, 3):
+        to = lax.rem(p.x + s, X)
+        qs.append(copies(cq.at[to], dq_slots.at[p.x], p.in_plane(to * C + p.c)))
+    put_q = pltpu.make_async_copy(cq.at[p.x], dq_slots.at[p.x], local.at[3])
     put_q.start()
     own_g.wait()
     for copy in zs:
@@ -352,20 +384,21 @@
             part = part + gy[g * members + i].astype(F32)
         both[:, g * DH : (g + 1) * DH] = part[:, :DH].astype(BF16)
         both[:, (KVG + g) * DH : (KVG + g + 1) * DH] = part[:, DH:].astype(BF16)
-    put_g = pltpu.make_async_copy(both, grads.at[at(p.slot, TOK)], local.at[3])
+    put_g = pltpu.make_async_copy(both, grads.at[mine], local.at[4])
     put_g.start()
-    run(plane_ring(copies, p, both, grads, TOK))
-    for copy in qs:
+    run(plane_ring(copies, p, both, whole(grads, TOK), TOK))
+    for copy in qs + hs:
         copy.wait_recv()
     copies.wait_sends()
-    put_q.wait()
-    put_g.wait()
-
-
-def finish_kernel(part, weights, raw, sums, rz, buf, send, recv, local):
+    for put in (put_h, put_q, put_g):
+        put.wait()
+
+
+def finish_kernel(part, weights, raw, sums, rz, ysum, send, recv, local):
     p = Place()
     rows = part.shape[0]
     piece = rows // Z
+    width = raw.shape[1]
     own = pltpu.make_async_copy(part.at[at(p.z, piece)], rz.at[p.z], local.at[0])
     own.start()
     barrier(plane_peers(p) + column_peers(p) + row_peers(p))
@@ -380,27 +413,47 @@
     total = rz[0].astype(F32)
     for z in range(1, Z):
         total = total + rz[z].astype(F32)
-    where = lambda z: buf.at[pl.ds(pl.multiple_of(p.slot * rows + z * piece, 16), piece)]
-    mine = pl.ds(pl.multiple_of(p.slot * rows + p.z * piece, 16), piece)
-    buf[mine, :] = total.astype(BF16)
-    run(column_ring(copies, p, where(p.z), where))
-    run(plane_ring(copies, p, buf.at[at(p.slot, rows)], buf, rows))
-    put = pltpu.make_async_copy(buf, raw, local.at[1])
-    put.start()
-    width = buf.shape[1]
-
-    def step(i, acc):
-        block = buf[pl.ds(pl.multiple_of(i * 64, 64), 64), :].astype(F32)
-        return acc + jnp.sum((block * block).reshape(8, 8, width), axis=0)
-
-    acc = lax.fori_loop(0, buf.shape[0] // 64, step, jnp.zeros((8, width), F32))
+
+    def where(slot, z, offset=0, count=piece):
+        return pl.ds(pl.multiple_of(slot * rows + z * piece + offset, 16), count)
+
+    raw[where(p.slot, p.z), :] = total.astype(BF16)
+    column = column_ring(copies, p, raw.at[where(p.slot, p.z)], lambda z: raw.at[where(p.slot, z)])
+    next(column)
+
+    def ring(z):
+        made = plane_ring(
+            copies,
+            p,
+            raw.at[where(p.slot, z)],
+            lambda slot, offset, count: raw.at[where(slot, z, offset, count)],
+            piece,
+        )
+        next(made)
+        return made
+
+    waves = [[ring(p.z)]]
+    for s in range(1, Z // 2 + 1):
+        next(column, None)
+        waves.append([ring(p.zslot(d)) for d in ((-s, s) if s < Z // 2 else (-s,))])
+        for wave in waves[max(0, s - 2) : s][::-1]:
+            for made in wave:
+                next(made)
+    square = sum_squares(raw.at[at(p.slot, rows)])
     row = lax.broadcasted_iota(jnp.int32, (8, width), 0)
-    sums[p.y] = jnp.where(row == 0, jnp.sum(acc, axis=0, keepdims=True), weights[...])
-    ys = [copies(sums.at[p.y], sums.at[p.y], peer) for peer in row_peers(p)]
+    ysum[p.y] = jnp.where(row == 0, square, weights[...])
+    ys = [copies(ysum.at[p.y], ysum.at[p.y], peer) for peer in row_peers(p)]
+    for wave in waves[Z // 2 - 1 :]:
+        for made in wave:
+            next(made)
     for copy in ys:
         copy.wait_recv()
+    sums[p.slot] = ysum[0] + ysum[1] + ysum[2] + ysum[3]
+    shares = [copies(sums.at[p.slot], sums.at[p.slot], peer) for peer in plane_peers(p)]
+    run(*[made for wave in waves for made in wave])
+    for copy in shares:
+        copy.wait_recv()
     copies.wait_sends()
-    put.wait()
 
 
 def remote(ident, kernel, **kw):
@@ -429,7 +482,7 @@
     piece = model // G
     columns = KVG * DH
     pos = jnp.broadcast_to(positions[None, :], (8, TOK))
-    qg, dog, kg, vg, hg, pg = remote(
+    qg, dog, kg, vg, pg, weights = remote(
         0,
         gather_kernel,
         out_shape=(
@@ -437,23 +490,24 @@
             shape((ROWS, width)),
             shape((Z * TOK, DH)),
             shape((Z * TOK, DH)),
-            shape((ROWS, piece)),
             shape((G, 8, TOK), jnp.int32),
+            shape((8, 2 * columns), F32),
         ),
-        in_specs=[ANY] * 6,
-        out_specs=(ANY,) * 6,
+        in_specs=[ANY] * 7,
+        out_specs=(ANY,) * 5 + (VMEM,),
         scratch_shapes=[
             pltpu.VMEM((TOK, width), BF16),
             pltpu.VMEM((TOK, width), BF16),
             pltpu.VMEM((TOK, DH), BF16),
             pltpu.VMEM((TOK, DH), BF16),
-            pltpu.VMEM((TOK, piece), BF16),
             pltpu.VMEM((8, TOK), jnp.int32),
-            dma(64),
-            dma(64),
+            pltpu.VMEM((model, columns), BF16),
+            pltpu.VMEM((model, columns), BF16),
+            dma(48),
+            dma(48),
             dma(12),
         ],
-    )(queries, out_grad, keys, values, hidden, pos)
+    )(queries, out_grad, keys, values, pos, key_weight, value_weight)
     tile = 256
     q_spec = pl.BlockSpec((tile, width), lambda j: (j, 0))
     k_spec = pl.BlockSpec((Z * TOK, DH), lambda j: (0, 0))
@@ -501,45 +555,44 @@
         ],
         compiler_params=params,
     )(stretch_owner, pg, shared, qg, dog, kg, vg)
-    dq_slots, grads = remote(
+    dq_slots, grads, hg = remote(
         2,
         reduce_kernel,
-        out_shape=(shape((G, TOK, width)), shape((ROWS, 2 * columns))),
-        in_specs=[ANY, ANY],
-        out_specs=(ANY, ANY),
+        out_shape=(shape((X, TOK, width)), shape((ROWS, 2 * columns)), shape((ROWS, piece))),
+        in_specs=[ANY, ANY, ANY],
+        out_specs=(ANY, ANY, ANY),
         scratch_shapes=[
-            pltpu.VMEM((TOK, width), BF16),
+            pltpu.VMEM((TOK, piece), BF16),
+            pltpu.VMEM((X, TOK, width), BF16),
+            pltpu.VMEM((X, TOK, width), BF16),
+            pltpu.VMEM((X, TOK, width), BF16),
             pltpu.VMEM((Z, TOK, 2 * DH), BF16),
             pltpu.VMEM((TOK, 2 * DH), BF16),
             pltpu.VMEM((Y, TOK, 2 * DH), BF16),
             pltpu.VMEM((TOK, 2 * columns), BF16),
             dma(40),
             dma(40),
-            dma(4),
+            dma(9),
         ],
-    )(dq, dkv)
+    )(dq, dkv, hidden)
     query_grad = jnp.sum(dq_slots.astype(F32), axis=0).astype(BF16)
     part = lax.dot_general(hg, grads, FIRST, preferred_element_type=F32).astype(BF16)
-    key_f = key_weight.astype(F32)
-    value_f = value_weight.astype(F32)
-    weight_sq = jnp.concatenate([jnp.sum(key_f * key_f, axis=0), jnp.sum(value_f * value_f, axis=0)])
     raw, sums = remote(
         3,
         finish_kernel,
-        out_shape=(shape((model, 2 * columns)), shape((Y, 8, 2 * columns), F32)),
+        out_shape=(shape((model, 2 * columns)), shape((G, 8, 2 * columns), F32)),
         in_specs=[ANY, VMEM],
-        out_specs=(ANY, VMEM),
+        out_specs=(VMEM, VMEM),
         scratch_shapes=[
             pltpu.VMEM((Z, piece // Z, 2 * columns), BF16),
-            pltpu.VMEM((model, 2 * columns), BF16),
-            dma(40),
-            dma(40),
-            dma(2),
+            pltpu.VMEM((Y, 8, 2 * columns), F32),
+            dma(112),
+            dma(112),
+            dma(1),
         ],
-    )(part, jnp.broadcast_to(weight_sq[None, :], (8, 2 * columns)))
-    total = jnp.sum(sums, axis=0)
-    grad_norm = jnp.sqrt(total[0] + EPSILON)
-    weight_norm = jnp.sqrt(total[1] + EPSILON)
+    )(part, weights)
+    grad_norm = jnp.sqrt(jnp.sum(sums[:, 0], axis=0) + EPSILON)
+    weight_norm = jnp.sqrt(sums[0, 1] + EPSILON)
     tokens = TOK * PAIRS
     factor = jnp.minimum(1.0, CLIP_RATE * tokens * weight_norm / grad_norm)
     key_out = raw[:, :columns].astype(F32) * factor[None, :columns]

time: 137 us -> 136 us (level)
  local copies, waits for them, and re-layouts: 0.04 us -> 6.61 us
  Pallas kernels: 131 us -> 125 us
  other arithmetic: 5.22 us -> 3.08 us
    unnamed x14 -> x16, local copies, waits for them, and re-layouts: 0.03 us -> 5.94 us
    pallas_call x2, Pallas kernels: 73.3 us -> 69.5 us  [the longest x1 35.3 us: local(): remote(3, finish_kernel, out_shape=(shape((model, 2 * columns)), shape((G...]
    pallas_call x1, Pallas kernels: 26.4 us -> 24.1 us  [local(): remote(0, gather_kernel, out_shape=(shape((ROWS, width)), shape((ROWS, wi...]
    reduce_sum x2 -> x1, other arithmetic: 2.09 us -> 0.03 us  [local(): grad_norm = jnp.sqrt(jnp.sum(sums[:, 0], axis=0) + EPSILON)]
where the time goes in v2:
time: 136 us
  Pallas kernels  125 us (92%)
  local copies, waits for them, and re-layouts  6.61 us (5%)
  other arithmetic  3.08 us (2%)
    pallas_call x1, Pallas kernels, local(): remote(3, finish_kernel, out_shape=(shape((model, 2 * columns)), shape((G...  35.3 us
    pallas_call x1, Pallas kernels, local(): remote(2, reduce_kernel, out_shape=(shape((X, TOK, width)), shape((ROWS,...  34.2 us
    pallas_call x1, Pallas kernels, local(): remote(0, gather_kernel, out_shape=(shape((ROWS, width)), shape((ROWS, wi...  24.1 us
    pallas_call x1, Pallas kernels, local(): pl.pallas_call(grads_kernel, grid=(ROWS // tile,), out_shape=(shape((ROWS...  13.4 us
    pallas_call x1, Pallas kernels, local(): remote(1, share_kernel, out_shape=shape((G, 2 * HEADS, ROWS), F32), in_sp...  9.7 us
    pallas_call x1, Pallas kernels, local(): pl.pallas_call(stats_kernel, grid=(ROWS // tile,), out_shape=shape((2 * H...  8.54 us
    unnamed x16, local copies, waits for them, and re-layouts  5.94 us

profile of v2, /device:TPU:1, one launch (start us, length us, event | category | flops | bytes accessed | tf_op | source)
XLA Modules:
  0.0 136.1 jit_solution(7294115083417728731)
XLA Ops:
  0.6 0.0 copy-start.7
  0.6 0.7 broadcast_in_dim.2.pos
  1.3 0.0 copy-start
  1.3 1.2 copy-done
  2.5 0.0 copy-start.1
  2.5 1.2 copy-done.1
  3.8 0.0 copy-start.3
  3.8 0.9 copy-done.3
  4.7 0.0 copy-start.4
  4.7 0.9 copy-done.4
  5.6 0.8 copy-done.5
  6.4 0.8 copy-done.6
  7.2 24.1 %shard_map.112 = (bf16[1024,512]{1,0:T(8,128)(2,1)S(1)}, bf16[1024,512]{1,0:T(8,128)(2,1)S(1)}, bf16[1024,128]{1,0:T(8,128)(2,1)S(1)}, bf16[1024,128]{1,0:T(8,12...) custom-call(bf16[128,512]{1,0:T(8,128)(2,1)S(1)} %copy-done.3, bf16[128,512]{1,0:T(8,128)(2,1)S(1)} %copy-done.4, ...), custom_call_target="tpu_custom_call" | custom-call | tf_op jit(solution)/shard_map/pallas_call | solution.py:485
  31.3 0.0 copy-done.7
  31.4 8.5 %shard_map.113.stats = f32[8,1024]{1,0:T(8,128)S(1)} custom-call(s32[64]{0:T(128)S(1)} %copy-done.7, s32[8,8,128]{2,1,0:T(8,128)S(1)} %get-tuple-element.16.pos, bf16[1024,512]{1,0:T(8,128)(2,1)S(1)} %get-tuple-element.17.q, bf16[1024,512]{1,0:T(8,128)(2,1)S(1)} %get-tuple-element.18.do, bf16[1024,128]{1,0:T(8,128)(2,1)S(1)} %get-tuple-element.19.k, ...), custom_call_target="tpu_custom_call" | custom-call | tf_op jit(solution)/shard_map/pallas_call | solution.py:518
  39.9 0.0 copy-start.2
  39.9 9.7 %shard_map.114.stats = f32[8,8,1024]{2,1,0:T(8,128)S(1)} custom-call(f32[8,1024]{1,0:T(8,128)S(1)} %shard_map.113.stats), custom_call_target="tpu_custom_call" | custom-call | tf_op jit(solution)/shard_map/pallas_call | solution.py:527
  49.6 13.4 %shard_map.115 = (bf16[1024,512]{1,0:T(8,128)(2,1)S(1)}, bf16[1024,256]{1,0:T(8,128)(2,1)S(1)}) custom-call(s32[64]{0:T(128)S(1)} %copy-done.7, s32[8,8,128]{2,1,0:T(8,128)S(1)} %get-tuple-element.16.pos, f32[8,8,1024]{2,1,0:T(8,128)S(1)} %shard_map.114.stats, bf16[1024,512]{1,0:T(8,128)(2,1)S(1)} %get-tuple-element.17.q, ...), custom_call_target="tpu_custom_call" | custom-call | tf_op jit(solution)/shard_map/pallas_call | solution.py:535
  63.0 0.0 copy-done.2
  63.0 34.2 %shard_map.116 = (bf16[4,128,512]{2,1,0:T(8,128)(2,1)S(1)}, bf16[1024,512]{1,0:T(8,128)(2,1)S(1)}, bf16[1024,256]{1,0:T(8,128)(2,1)S(1)}) custom-call(bf16[1024,512]{1,0:T(8,128)(2,1)S(1)} %get-tuple-element.21.dq, bf16[1024,256]{1,0:T(8,128)(2,1)S(1)} %get-tuple-element.22.dkv, bf16[128,2048]{1,0:T(8,128)(2,1)S(1)} %copy-done.2), custom_call_target="tpu_custom_call" | custom-call | tf_op jit(solution)/shard_map/pallas_call | solution.py:558
  97.3 0.7 reduce_sum.21
  98.0 0.5 convolution_convert_fusion.part
  98.5 35.3 %shard_map.117 = (bf16[2048,512]{1,0:T(8,128)(2,1)S(1)}, f32[8,8,512]{2,1,0:T(8,128)S(1)}) custom-call(bf16[256,512]{1,0:T(8,128)(2,1)S(1)} %convolution_convert_fusion.part, f32[8,512]{1,0:T(8,128)S(1)} %get-tuple-element.26.weights), custom_call_target="tpu_custom_call" | custom-call | tf_op jit(solution)/shard_map/pallas_call | solution.py:580
  133.8 2.3 %convert_multiply_fusion = (f32[2048,256]{1,0:T(8,128)}, f32[2048,256]{1,0:T(8,128)}) fusion(f32[256]{0:T(256)S(1)} %get-tuple-element.31, bf16[2048,512]{1,0:T(8,128)(2,1)S(1)} %get-tuple-element.27, f32[256]{0:T(256)S(1)} %get-tuple-element.32), kind=kLoop, calls=%fused_computation | loop fusion | flops 2097152 | bytes 6293504 | tf_op jit(solution)/shard_map/mul | solution.py:599
  (6 shorter events, 0.1 us)
Async XLA Ops:
  0.6 30.7 %copy-start.7 = (s32[64]{0:T(128)S(1)}, s32[64]{0:T(128)}, u32[]{:S(2)}) copy-start(s32[64]{0:T(128)} %owners.3) | copy-start | bytes 772
  1.3 1.2 copy-start
  2.5 1.2 copy-start.1
  3.8 0.9 copy-start.3
  4.7 0.9 copy-start.4
  5.6 0.8 copy-start.5
  6.4 0.8 copy-start.6
  39.9 23.1 %copy-start.2 = (bf16[128,2048]{1,0:T(8,128)(2,1)S(1)}, bf16[128,2048]{1,0:T(8,128)(2,1)}, u32[]{:S(2)}) copy-start(bf16[128,2048]{1,0:T(8,128)(2,1)} %hid.1) | copy-start | bytes 1572868

commit v3 on v2

--- a/solution.py
+++ b/solution.py
@@ -29,6 +29,7 @@
 MESH = pl.DeviceIdType.MESH
 ANY = pl.BlockSpec(memory_space=pl.ANY)
 VMEM = pl.BlockSpec(memory_space=pltpu.VMEM)
+HBM = pl.BlockSpec(memory_space=pltpu.HBM)
 SMEM = pl.BlockSpec(memory_space=pltpu.SMEM)
 LAST = (((1,), (1,)), ((), ()))
 FIRST = (((0,), (0,)), ((), ()))
@@ -179,9 +180,7 @@
     return jnp.sum(acc, axis=0, keepdims=True)
 
 
-def gather_kernel(
-    q, do, k, v, pos, kw, vw, qg, dog, kg, vg, pg, wsum, tq, tdo, tk, tv, tp, tkw, tvw, send, recv, local
-):
+def gather_kernel(q, do, k, v, pos, qg, dog, kg, vg, pg, tq, tdo, tk, tv, send, recv, local):
     p = Place()
     group = lax.div(p.y * HEADS, HPG)
     cols = pl.ds(pl.multiple_of(group * DH, DH), DH)
@@ -192,26 +191,18 @@
         (do, tdo, dog.at[mine]),
         (own_k, tk, kg.at[at(p.z, TOK)]),
         (own_v, tv, vg.at[at(p.z, TOK)]),
-        (pos, tp, pg.at[p.slot]),
     ]
     loads = [pltpu.make_async_copy(s, t, local.at[i]) for i, (s, t, _) in enumerate(moves)]
     for load in loads:
         load.start()
-    heavy = [
-        pltpu.make_async_copy(s, t, local.at[2 * len(moves) + i])
-        for i, (s, t) in enumerate(((kw, tkw), (vw, tvw)))
-    ]
-    for load in heavy:
-        load.start()
+    pg[p.slot] = jnp.broadcast_to(pos[...], (8, TOK))
     barrier(plane_peers(p) + [p.in_column(p.zslot(1)), p.in_column(p.zslot(-1))])
     copies = Copies(send, recv)
-    rings = [
-        column_ring(copies, p, own_k, lambda z: kg.at[at(z, TOK)]),
-        plane_ring(copies, p, q, whole(qg, TOK), TOK),
-        column_ring(copies, p, own_v, lambda z: vg.at[at(z, TOK)]),
-        plane_ring(copies, p, do, whole(dog, TOK), TOK),
-    ]
-    for ring in rings:
+    kr = column_ring(copies, p, own_k, lambda z: kg.at[at(z, TOK)])
+    vr = column_ring(copies, p, own_v, lambda z: vg.at[at(z, TOK)])
+    qr = plane_ring(copies, p, q, whole(qg, TOK), TOK)
+    dr = plane_ring(copies, p, do, whole(dog, TOK), TOK)
+    for ring in (kr, vr, qr, dr):
         next(ring)
     stores = []
     for i, (_, t, d) in enumerate(moves):
@@ -219,13 +210,10 @@
         store = pltpu.make_async_copy(t, d, local.at[len(moves) + i])
         store.start()
         stores.append(store)
-    small = [copies(pos, pg.at[p.slot], peer) for peer in plane_peers(p)]
-    for load in heavy:
-        load.wait()
-    wsum[...] = jnp.broadcast_to(
-        jnp.concatenate([sum_squares(tkw), sum_squares(tvw)], axis=1), wsum.shape
-    )
-    run(*rings)
+    small = [copies(pg.at[p.slot], pg.at[p.slot], peer) for peer in plane_peers(p)]
+    for ring in (kr, vr, kr, vr, qr, kr, vr, dr, kr, vr, qr, dr):
+        next(ring, None)
+    run(qr, dr)
     for copy in small:
         copy.wait_recv()
     copies.wait_sends()
@@ -283,7 +271,7 @@
     load.wait()
 
 
-def grads_kernel(owners, pos, stats, q, do, k, v, dq, dkv, bias, kt, probs, slopes, acc):
+def grads_kernel(owners, pos, stats, q, do, k, v, dq, dk, dv, bias, kt, probs, slopes, acc):
     p = Place()
     j = pl.program_id(0)
     width = q.shape[0]
@@ -317,45 +305,120 @@
 
     @pl.when(j == pl.num_programs(0) - 1)
     def _():
-        dkv[:, :DH] = (acc[:, :DH] * SCALE).astype(BF16)
-        dkv[:, DH:] = acc[:, DH:].astype(BF16)
-
-
-def reduce_kernel(
-    dq, dkv, hid, dq_slots, grads, hg, th, dqa, pq, cq, gz, ysend, gy, both, send, recv, local
+        dk[...] = (acc[:, :DH] * SCALE).astype(BF16)
+        dv[...] = acc[:, DH:].astype(BF16)
+
+
+FARTHEST = (4, 3, 5, 2, 6, 1, 7)
+
+
+def rounded_sum(ref, i, count):
+    total = ref[i, 0].astype(F32)
+    for n in range(1, count):
+        total = total + ref[i, n].astype(F32)
+    return total.astype(BF16)
+
+
+def tail_kernel(
+    dq, dk, dv, hid, kw, vw, dq_slots, raw_k, raw_v, sums,
+    hg, hgt, dqa, pq, cq, gz, gy, grads, part, rz, ysum, wsum, tw, send, recv, local
 ):
     p = Place()
     wide = hid.shape[1] // G
+    piece = wide // Z
     mine = at(p.slot, TOK)
+    members = Y // KVG
 
     def strip(slot):
         return hid.at[:, pl.ds(pl.multiple_of(slot * wide, 128), wide)]
 
-    own_h = pltpu.make_async_copy(strip(p.slot), th, local.at[0])
-    own_h.start()
-    own_g = pltpu.make_async_copy(dkv.at[at(p.z, TOK)], gz.at[p.z], local.at[1])
-    own_g.start()
     kept = [
-        pltpu.make_async_copy(dq.at[at(x * C + p.c, TOK)], dqa.at[x], local.at[5 + x])
+        pltpu.make_async_copy(dq.at[at(x * C + p.c, TOK)], dqa.at[x], local.at[x])
         for x in range(X)
     ]
-    for load in kept:
+    own_g = [
+        pltpu.make_async_copy(src.at[at(p.z, TOK)], gz.at[i, p.z], local.at[X + i])
+        for i, src in enumerate((dk, dv))
+    ]
+    own_h = pltpu.make_async_copy(strip(p.slot), hg.at[mine], local.at[X + 2])
+    loads = [pltpu.make_async_copy(w, tw.at[i], local.at[X + 3 + i]) for i, w in enumerate((kw, vw))]
+    for load in kept + own_g + [own_h] + loads:
         load.start()
     barrier(plane_peers(p) + column_peers(p) + row_peers(p))
     copies = Copies(send, recv)
-    zs = [
-        copies(dkv.at[at(p.zslot(s), TOK)], gz.at[p.z], p.in_column(p.zslot(s)))
-        for s in (4, 3, 5, 2, 6, 1, 7)
-    ]
+
+    def stream(i, src, raw):
+        made = [
+            copies(src.at[at(p.zslot(s), TOK)], gz.at[i, p.z], p.in_column(p.zslot(s)))
+            for s in FARTHEST
+        ]
+        yield
+        own_g[i].wait()
+        for copy in made:
+            copy.wait_recv()
+        gy[i, p.y] = rounded_sum(gz, i, Z)
+        made = [copies(gy.at[i, p.y], gy.at[i, p.y], peer) for peer in row_peers(p)]
+        yield
+        for copy in made:
+            copy.wait_recv()
+        for g in range(KVG):
+            total = gy[i, g * members].astype(F32)
+            for n in range(1, members):
+                total = total + gy[i, g * members + n].astype(F32)
+            grads[i, mine, g * DH : (g + 1) * DH] = total.astype(BF16)
+        ring = plane_ring(copies, p, grads.at[i, mine], whole(grads.at[i], TOK), TOK)
+        for _ in ring:
+            yield
+        product = jnp.dot(hgt[...], grads[i], preferred_element_type=F32)
+        part[i] = product.astype(BF16)
+        rz[i, p.z] = part[i, at(p.z, piece), :]
+        made = [
+            copies(part.at[i, at(p.zslot(s), piece)], rz.at[i, p.z], p.in_column(p.zslot(s)))
+            for s in FARTHEST
+        ]
+        yield
+        for copy in made:
+            copy.wait_recv()
+        own = pl.ds(pl.multiple_of(p.slot * wide + p.z * piece, 16), piece)
+        raw[own, :] = rounded_sum(rz, i, Z)
+        made = [
+            copies(raw.at[own], raw.at[own], p.in_column(p.zslot(s))) for s in FARTHEST
+        ]
+        yield
+        for copy in made:
+            copy.wait_recv()
+        ring = plane_ring(copies, p, raw.at[at(p.slot, wide)], whole(raw, wide), wide)
+        next(ring)
+        square = sum_squares(raw.at[at(p.slot, wide)])
+        row = lax.broadcasted_iota(jnp.int32, (8, square.shape[1]), 0)
+        ysum[i, p.y] = jnp.where(row == 0, square, wsum[i])
+        made = [copies(ysum.at[i, p.y], ysum.at[i, p.y], peer) for peer in row_peers(p)]
+        yield
+        next(ring)
+        for copy in made:
+            copy.wait_recv()
+        total = ysum[i, 0]
+        for n in range(1, Y):
+            total = total + ysum[i, n]
+        sums[i, p.slot] = total
+        made = [copies(sums.at[i, p.slot], sums.at[i, p.slot], peer) for peer in plane_peers(p)]
+        yield
+        next(ring)
+        yield
+        for _ in ring:
+            pass
+        for copy in made:
+            copy.wait_recv()
+
+    streams = [stream(0, dk, raw_k), stream(1, dv, raw_v)]
+    for one in streams:
+        next(one)
     partner = p.in_plane(p.xslot(0, True))
     given = [copies(dq.at[at(x * C + 1 - p.c, TOK)], pq.at[x], partner) for x in range(X)]
     hs = []
     for s, f in ((2, False), (2, True), (1, False), (3, False), (1, True), (3, True), (0, True)):
         to = p.xslot(s, f)
         hs.append(copies(strip(to), hg.at[mine], p.in_plane(to)))
-    own_h.wait()
-    put_h = pltpu.make_async_copy(th, hg.at[mine], local.at[2])
-    put_h.start()
     for x in range(X):
         kept[x].wait()
         given[x].wait_recv()
@@ -364,96 +427,22 @@
     for s in (2, 1, 3):
         to = lax.rem(p.x + s, X)
         qs.append(copies(cq.at[to], dq_slots.at[p.x], p.in_plane(to * C + p.c)))
-    put_q = pltpu.make_async_copy(cq.at[p.x], dq_slots.at[p.x], local.at[3])
+    put_q = pltpu.make_async_copy(cq.at[p.x], dq_slots.at[p.x], local.at[X + 5])
     put_q.start()
-    own_g.wait()
-    for copy in zs:
+    for i, load in enumerate(loads):
+        load.wait()
+        wsum[i] = jnp.broadcast_to(sum_squares(tw.at[i]), wsum.shape[1:])
+    for one in streams:
+        next(one)
+    own_h.wait()
+    for copy in hs:
         copy.wait_recv()
-    total = gz[0].astype(F32)
-    for z in range(1, Z):
-        total = total + gz[z].astype(F32)
-    ysend[...] = total.astype(BF16)
-    gy[p.y] = total.astype(BF16)
-    ys = [copies(ysend, gy.at[p.y], peer) for peer in row_peers(p)]
-    for copy in ys:
-        copy.wait_recv()
-    members = Y // KVG
-    for g in range(KVG):
-        part = gy[g * members].astype(F32)
-        for i in range(1, members):
-            part = part + gy[g * members + i].astype(F32)
-        both[:, g * DH : (g + 1) * DH] = part[:, :DH].astype(BF16)
-        both[:, (KVG + g) * DH : (KVG + g + 1) * DH] = part[:, DH:].astype(BF16)
-    put_g = pltpu.make_async_copy(both, grads.at[mine], local.at[4])
-    put_g.start()
-    run(plane_ring(copies, p, both, whole(grads, TOK), TOK))
-    for copy in qs + hs:
+    hgt[...] = hg[...].T
+    run(*streams)
+    for copy in qs:
         copy.wait_recv()
     copies.wait_sends()
-    for put in (put_h, put_q, put_g):
-        put.wait()
-
-
-def finish_kernel(part, weights, raw, sums, rz, ysum, send, recv, local):
-    p = Place()
-    rows = part.shape[0]
-    piece = rows // Z
-    width = raw.shape[1]
-    own = pltpu.make_async_copy(part.at[at(p.z, piece)], rz.at[p.z], local.at[0])
-    own.start()
-    barrier(plane_peers(p) + column_peers(p) + row_peers(p))
-    copies = Copies(send, recv)
-    zs = [
-        copies(part.at[at(p.zslot(s), piece)], rz.at[p.z], p.in_column(p.zslot(s)))
-        for s in (4, 3, 5, 2, 6, 1, 7)
-    ]
-    own.wait()
-    for copy in zs:
-        copy.wait_recv()
-    total = rz[0].astype(F32)
-    for z in range(1, Z):
-        total = total + rz[z].astype(F32)
-
-    def where(slot, z, offset=0, count=piece):
-        return pl.ds(pl.multiple_of(slot * rows + z * piece + offset, 16), count)
-
-    raw[where(p.slot, p.z), :] = total.astype(BF16)
-    column = column_ring(copies, p, raw.at[where(p.slot, p.z)], lambda z: raw.at[where(p.slot, z)])
-    next(column)
-
-    def ring(z):
-        made = plane_ring(
-            copies,
-            p,
-            raw.at[where(p.slot, z)],
-            lambda slot, offset, count: raw.at[where(slot, z, offset, count)],
-            piece,
-        )
-        next(made)
-        return made
-
-    waves = [[ring(p.z)]]
-    for s in range(1, Z // 2 + 1):
-        next(column, None)
-        waves.append([ring(p.zslot(d)) for d in ((-s, s) if s < Z // 2 else (-s,))])
-        for wave in waves[max(0, s - 2) : s][::-1]:
-            for made in wave:
-                next(made)
-    square = sum_squares(raw.at[at(p.slot, rows)])
-    row = lax.broadcasted_iota(jnp.int32, (8, width), 0)
-    ysum[p.y] = jnp.where(row == 0, square, weights[...])
-    ys = [copies(ysum.at[p.y], ysum.at[p.y], peer) for peer in row_peers(p)]
-    for wave in waves[Z // 2 - 1 :]:
-        for made in wave:
-            next(made)
-    for copy in ys:
-        copy.wait_recv()
-    sums[p.slot] = ysum[0] + ysum[1] + ysum[2] + ysum[3]
-    shares = [copies(sums.at[p.slot], sums.at[p.slot], peer) for peer in plane_peers(p)]
-    run(*[made for wave in waves for made in wave])
-    for copy in shares:
-        copy.wait_recv()
-    copies.wait_sends()
+    put_q.wait()
 
 
 def remote(ident, kernel, **kw):
@@ -481,8 +470,7 @@
     model = hidden.shape[1]
     piece = model // G
     columns = KVG * DH
-    pos = jnp.broadcast_to(positions[None, :], (8, TOK))
-    qg, dog, kg, vg, pg, weights = remote(
+    qg, dog, kg, vg, pg = remote(
         0,
         gather_kernel,
         out_shape=(
@@ -491,23 +479,19 @@
             shape((Z * TOK, DH)),
             shape((Z * TOK, DH)),
             shape((G, 8, TOK), jnp.int32),
-            shape((8, 2 * columns), F32),
         ),
-        in_specs=[ANY] * 7,
-        out_specs=(ANY,) * 5 + (VMEM,),
+        in_specs=[HBM] * 4 + [VMEM],
+        out_specs=(ANY,) * 4 + (VMEM,),
         scratch_shapes=[
             pltpu.VMEM((TOK, width), BF16),
             pltpu.VMEM((TOK, width), BF16),
             pltpu.VMEM((TOK, DH), BF16),
             pltpu.VMEM((TOK, DH), BF16),
-            pltpu.VMEM((8, TOK), jnp.int32),
-            pltpu.VMEM((model, columns), BF16),
-            pltpu.VMEM((model, columns), BF16),
             dma(48),
             dma(48),
-            dma(12),
+            dma(8),
         ],
-    )(queries, out_grad, keys, values, pos, key_weight, value_weight)
+    )(queries, out_grad, keys, values, positions.reshape(1, TOK))
     tile = 256
     q_spec = pl.BlockSpec((tile, width), lambda j: (j, 0))
     k_spec = pl.BlockSpec((Z * TOK, DH), lambda j: (0, 0))
@@ -532,10 +516,10 @@
         out_specs=VMEM,
         scratch_shapes=[dma(8), dma(8), dma(1)],
     )(stats)
-    dq, dkv = pl.pallas_call(
+    dq, dk, dv = pl.pallas_call(
         grads_kernel,
         grid=(ROWS // tile,),
-        out_shape=(shape((ROWS, width)), shape((Z * TOK, 2 * DH))),
+        out_shape=(shape((ROWS, width)), shape((Z * TOK, DH)), shape((Z * TOK, DH))),
         in_specs=[
             SMEM,
             pos_spec,
@@ -545,7 +529,7 @@
             k_spec,
             k_spec,
         ],
-        out_specs=(q_spec, pl.BlockSpec((Z * TOK, 2 * DH), lambda j: (0, 0))),
+        out_specs=(q_spec, k_spec, k_spec),
         scratch_shapes=[
             pltpu.VMEM((Z * TOK, tile), F32),
             pltpu.VMEM((DH, Z * TOK), BF16),
@@ -555,49 +539,46 @@
         ],
         compiler_params=params,
     )(stretch_owner, pg, shared, qg, dog, kg, vg)
-    dq_slots, grads, hg = remote(
+    dq_slots, raw_k, raw_v, sums = remote(
         2,
-        reduce_kernel,
-        out_shape=(shape((X, TOK, width)), shape((ROWS, 2 * columns)), shape((ROWS, piece))),
-        in_specs=[ANY, ANY, ANY],
-        out_specs=(ANY, ANY, ANY),
+        tail_kernel,
+        out_shape=(
+            shape((X, TOK, width)),
+            shape((model, columns)),
+            shape((model, columns)),
+            shape((2, G, 8, columns), F32),
+        ),
+        in_specs=[ANY] * 3 + [HBM] * 3,
+        out_specs=(ANY, VMEM, VMEM, VMEM),
         scratch_shapes=[
-            pltpu.VMEM((TOK, piece), BF16),
+            pltpu.VMEM((ROWS, piece), BF16),
+            pltpu.VMEM((piece, ROWS), BF16),
             pltpu.VMEM((X, TOK, width), BF16),
             pltpu.VMEM((X, TOK, width), BF16),
             pltpu.VMEM((X, TOK, width), BF16),
-            pltpu.VMEM((Z, TOK, 2 * DH), BF16),
-            pltpu.VMEM((TOK, 2 * DH), BF16),
-            pltpu.VMEM((Y, TOK, 2 * DH), BF16),
-            pltpu.VMEM((TOK, 2 * columns), BF16),
-            dma(40),
-            dma(40),
-            dma(9),
+            pltpu.VMEM((2, Z, TOK, DH), BF16),
+            pltpu.VMEM((2, Y, TOK, DH), BF16),
+            pltpu.VMEM((2, ROWS, columns), BF16),
+            pltpu.VMEM((2, piece, columns), BF16),
+            pltpu.VMEM((2, Z, piece // Z, columns), BF16),
+            pltpu.VMEM((2, Y, 8, columns), F32),
+            pltpu.VMEM((2, 8, columns), F32),
+            pltpu.VMEM((2, model, columns), BF16),
+            dma(128),
+            dma(128),
+            dma(10),
         ],
-    )(dq, dkv, hidden)
+    )(dq, dk, dv, hidden, key_weight, value_weight)
     query_grad = jnp.sum(dq_slots.astype(F32), axis=0).astype(BF16)
-    part = lax.dot_general(hg, grads, FIRST, preferred_element_type=F32).astype(BF16)
-    raw, sums = remote(
-        3,
-        finish_kernel,
-        out_shape=(shape((model, 2 * columns)), shape((G, 8, 2 * columns), F32)),
-        in_specs=[ANY, VMEM],
-        out_specs=(VMEM, VMEM),
-        scratch_shapes=[
-            pltpu.VMEM((Z, piece // Z, 2 * columns), BF16),
-            pltpu.VMEM((Y, 8, 2 * columns), F32),
-            dma(112),
-            dma(112),
-            dma(1),
-        ],
-    )(part, weights)
-    grad_norm = jnp.sqrt(jnp.sum(sums[:, 0], axis=0) + EPSILON)
-    weight_norm = jnp.sqrt(sums[0, 1] + EPSILON)
     tokens = TOK * PAIRS
-    factor = jnp.minimum(1.0, CLIP_RATE * tokens * weight_norm / grad_norm)
-    key_out = raw[:, :columns].astype(F32) * factor[None, :columns]
-    value_out = raw[:, columns:].astype(F32) * factor[None, columns:]
-    return (query_grad, key_out, value_out)
+
+    def clipped(i, raw):
+        grad_norm = jnp.sqrt(jnp.sum(sums[i, :, 0], axis=0) + EPSILON)
+        weight_norm = jnp.sqrt(sums[i, 0, 1] + EPSILON)
+        factor = jnp.minimum(1.0, CLIP_RATE * tokens * weight_norm / grad_norm)
+        return raw.astype(F32) * factor[None, :]
+
+    return (query_grad, clipped(0, raw_k), clipped(1, raw_v))
 
 
 def solution(mesh):

time: 136 us -> 122 us (0.90)
  Pallas kernels: 125 us -> 113 us
  local copies, waits for them, and re-layouts: 6.61 us -> 4.82 us
    pallas_call x2 -> x1, Pallas kernels: 69.5 us -> 58.6 us  [local(): remote(2, tail_kernel, out_shape=(shape((X, TOK, width)), shape((model, c...]
    pallas_call x1, Pallas kernels: 9.7 us -> 7.17 us  [local(): remote(1, share_kernel, out_shape=shape((G, 2 * HEADS, ROWS), F32), in_sp...]
    unnamed x16 -> x20, local copies, waits for them, and re-layouts: 5.94 us -> 4.82 us
where the time goes in v3:
time: 122 us; the launch traced here: 121 us
  Pallas kernels  113 us (93%)
  local copies, waits for them, and re-layouts  4.82 us (4%)
  other arithmetic  3.15 us (3%)
    pallas_call x1, Pallas kernels, local(): remote(2, tail_kernel, out_shape=(shape((X, TOK, width)), shape((model, c...  58.6 us
    pallas_call x1, Pallas kernels, local(): remote(0, gather_kernel, out_shape=(shape((ROWS, width)), shape((ROWS, wi...  25 us
    pallas_call x1, Pallas kernels, local(): pl.pallas_call(grads_kernel, grid=(ROWS // tile,), out_shape=(shape((ROWS...  13.4 us
    pallas_call x1, Pallas kernels, local(): pl.pallas_call(stats_kernel, grid=(ROWS // tile,), out_shape=shape((2 * H...  8.52 us
    pallas_call x1, Pallas kernels, local(): remote(1, share_kernel, out_shape=shape((G, 2 * HEADS, ROWS), F32), in_sp...  7.17 us
    unnamed x20, local copies, waits for them, and re-layouts  4.82 us

profile of v3, /device:TPU:1, one launch (start us, length us, event | category | flops | bytes accessed | tf_op | source)
XLA Modules:
  0.0 121.4 jit_solution(4950291444734049206)
XLA Ops:
  0.6 0.0 copy-start.8
  0.6 0.0 copy-start.3
  0.7 0.9 copy-done.3
  1.6 0.0 copy-start.4
  1.6 0.9 copy-done.4
  2.5 0.8 copy-done.5
  3.3 0.8 copy-done.6
  4.1 0.7 copy-done.9
  4.8 25.0 %shard_map.112 = (bf16[1024,512]{1,0:T(8,128)(2,1)S(1)}, bf16[1024,512]{1,0:T(8,128)(2,1)S(1)}, bf16[1024,128]{1,0:T(8,128)(2,1)S(1)}, bf16[1024,128]{1,0:T(8,128)(2,1)S(1)}, s32[8,8,128]{2,1,0:T(8,128)S(1)}) custom-call(bf16[128,512]{1,0:T(8,128)(2,1)S(1)} %copy-done.3, bf16[128,512]{1,0:T(8,128)(2,1)S(1)} %copy-done.4, bf16[128,256]{1,0:T(8,128)(2,1)S(1)} %copy-done.5, ...), custom_call_target="tpu_custom_call" | custom-call | tf_op jit(solution)/shard_map/pallas_call | solution.py:473
  29.8 0.0 copy-start.7
  29.8 0.6 copy-done.7
  30.5 8.5 %shard_map.113.stats = f32[8,1024]{1,0:T(8,128)S(1)} custom-call(s32[64]{0:T(128)S(1)} %copy-done.7, s32[8,8,128]{2,1,0:T(8,128)S(1)} %get-tuple-element.15.pos, bf16[1024,512]{1,0:T(8,128)(2,1)S(1)} %get-tuple-element.16.q, bf16[1024,512]{1,0:T(8,128)(2,1)S(1)} %get-tuple-element.17.do, bf16[1024,128]{1,0:T(8,128)(2,1)S(1)} %get-tuple-element.18.k, ...), custom_call_target="tpu_custom_call" | custom-call | tf_op jit(solution)/shard_map/pallas_call | solution.py:502
  39.0 0.0 copy-start
  39.0 0.0 copy-start.1
  39.0 0.0 copy-start.2
  39.0 7.2 %shard_map.114.stats = f32[8,8,1024]{2,1,0:T(8,128)S(1)} custom-call(f32[8,1024]{1,0:T(8,128)S(1)} %shard_map.113.stats), custom_call_target="tpu_custom_call" | custom-call | tf_op jit(solution)/shard_map/pallas_call | solution.py:511
  46.2 0.0 copy-done.8
  46.2 13.4 %shard_map.115 = (bf16[1024,512]{1,0:T(8,128)(2,1)S(1)}, bf16[1024,128]{1,0:T(8,128)(2,1)S(1)}, bf16[1024,128]{1,0:T(8,128)(2,1)S(1)}) custom-call(s32[64]{0:T(128)S(1)} %copy-done.8, s32[8,8,128]{2,1,0:T(8,128)S(1)} %get-tuple-element.15.pos, f32[8,8,1024]{2,1,0:T(8,128)S(1)} %shard_map.114.stats, bf16[1024,512]{1,0:T(8,128)(2,1)S(1)} %get-tuple-element.16.q, ...), custom_call_target="tpu_custom_call" | custom-call | tf_op jit(solution)/shard_map/pallas_call | solution.py:519
  59.6 0.0 copy-done
  59.6 0.0 copy-done.1
  59.6 0.0 copy-done.2
  59.6 58.6 %shard_map.116 = (bf16[4,128,512]{2,1,0:T(8,128)(2,1)S(1)}, bf16[2048,256]{1,0:T(8,128)(2,1)S(1)}, bf16[2048,256]{1,0:T(8,128)(2,1)S(1)}, f32[2,8,8,256]{3,2,1,0:T(8,128)S(1)}) custom-call(bf16[1024,512]{1,0:T(8,128)(2,1)S(1)} %get-tuple-element.20.dq, bf16[1024,128]{1,0:T(8,128)(2,1)S(1)} %get-tuple-element.21.dk, ...), custom_call_target="tpu_custom_call" | custom-call | tf_op jit(solution)/shard_map/pallas_call | solution.py:542
  118.2 0.7 reduce_sum.30
  119.1 2.3 %convert_multiply_fusion = (f32[2048,256]{1,0:T(8,128)}, f32[2048,256]{1,0:T(8,128)}) fusion(bf16[2048,256]{1,0:T(8,128)(2,1)S(1)} %get-tuple-element.26, f32[256]{0:T(256)S(1)} %multiply_minimum_fusion, f32[256]{0:T(256)S(1)} %multiply_minimum_fusion.1, bf16[2048,256]{1,0:T(8,128)(2,1)S(1)} %get-tuple-element.24), kind=kLoop, calls=%fused_computation | loop fusion | flops 2097152 | bytes 6293504 | tf_op jit(solution)/shard_map/mul | solution.py:579
  (7 shorter events, 0.1 us)
Async XLA Ops:
  0.6 45.6 %copy-start.8 = (s32[64]{0:T(128)S(1)}, s32[64]{0:T(128)}, u32[]{:S(2)}) copy-start(s32[64]{0:T(128)} %owners.3) | copy-start | bytes 772
  0.6 0.9 copy-start.3
  1.6 0.9 copy-start.4
  2.5 0.8 copy-start.5
  3.3 0.8 copy-start.6
  4.1 0.7 copy-start.9
  29.8 0.7 copy-start.7
  39.0 20.6 %copy-start = (bf16[2048,256]{1,0:T(8,128)(2,1)S(1)}, bf16[2048,256]{1,0:T(8,128)(2,1)}, u32[]{:S(2)}) copy-start(bf16[2048,256]{1,0:T(8,128)(2,1)} %kw.1) | copy-start | bytes 3145732
  39.0 20.6 %copy-start.1 = (bf16[2048,256]{1,0:T(8,128)(2,1)S(1)}, bf16[2048,256]{1,0:T(8,128)(2,1)}, u32[]{:S(2)}) copy-start(bf16[2048,256]{1,0:T(8,128)(2,1)} %vw.1) | copy-start | bytes 3145732
  39.0 20.6 %copy-start.2 = (bf16[128,2048]{1,0:T(8,128)(2,1)S(1)}, bf16[128,2048]{1,0:T(8,128)(2,1)}, u32[]{:S(2)}) copy-start(bf16[128,2048]{1,0:T(8,128)(2,1)} %hid.1) | copy-start | bytes 1572868

commit v4 on v3

v4 whole, which is shorter than its diff:
```python
import functools
import math

import jax
import jax.numpy as jnp
from jax import lax
from jax.experimental import pallas as pl
from jax.experimental.pallas import tpu as pltpu
from jax.sharding import PartitionSpec as P

DH = 128
HPG = 8
KVG = 2
TOK = 128
HALF = TOK // 2
Z = 8
X = 4
C = 2
Y = 4
G = X * C
PAIRS = Z * X * C
HEADS = 4
ROWS = G * TOK
CLIP_RATE = 0.02
TILE = 256
VMEM_BYTES = 62 * 1024 * 1024
EPSILON = 1e-06
NEGATIVE = -1e30
SCALE = 1.0 / math.sqrt(DH)
SCALE2 = SCALE * math.log2(math.e)
MESH = pl.DeviceIdType.MESH
ANY = pl.BlockSpec(memory_space=pl.ANY)
VMEM = pl.BlockSpec(memory_space=pltpu.VMEM)
HBM = pl.BlockSpec(memory_space=pltpu.HBM)
SMEM = pl.BlockSpec(memory_space=pltpu.SMEM)
LAST = (((1,), (1,)), ((), ()))
FIRST = (((0,), (0,)), ((), ()))
BF16 = jnp.bfloat16
F32 = jnp.float32


class Place:
    def __init__(self):
        me = lax.axis_index("ctx")
        self.me = me
        self.y = lax.axis_index("fsdp")
        self.z = lax.div(me, G)
        self.slot = lax.rem(me, G)
        self.x = lax.div(self.slot, C)
        self.c = lax.rem(self.slot, C)

    def xslot(self, step, flip=False):
        x = lax.rem(self.x + step + X, X)
        return x * C + ((1 - self.c) if flip else self.c)

    def in_plane(self, slot):
        return {"ctx": self.z * G + slot}

    def zslot(self, step):
        return lax.rem(self.z + step + Z, Z)

    def in_column(self, z):
        return {"ctx": z * G + self.slot}

    def yslot(self, step):
        return lax.rem(self.y + step, Y)


class Copies:
    def __init__(self, send, recv):
        self.send, self.recv, self.made = send, recv, []

    def __call__(self, src, dst, device):
        i = len(self.made)
        copy = pltpu.make_async_remote_copy(
            src_ref=src,
            dst_ref=dst,
            send_sem=self.send.at[i],
            recv_sem=self.recv.at[i],
            device_id=device,
            device_id_type=MESH,
        )
        copy.start()
        self.made.append(copy)
        return copy

    def wait_sends(self):
        for copy in self.made:
            copy.wait_send()


def barrier(devices):
    sem = pltpu.get_barrier_semaphore()
    for device in devices:
        pl.semaphore_signal(sem, inc=1, device_id=device, device_id_type=MESH)
    pl.semaphore_wait(sem, len(devices))


def at(slot, rows, offset=0, count=None):
    return pl.ds(pl.multiple_of(slot * rows + offset, 16), rows if count is None else count)


def plane_ring(copies, p, src, where, rows):
    half = rows // 2
    right, left = p.xslot(1), p.xslot(-1)
    far = p.xslot(2)
    partner = p.in_plane(p.xslot(0, True))
    mine = where(p.slot, 0, rows)
    a = copies(src, mine, p.in_plane(right))
    b = copies(src, mine, p.in_plane(left))
    own = copies(src, mine, partner)
    yield
    a.wait_recv()
    first = where(left, 0, half)
    f = copies(first, first, p.in_plane(right))
    block = where(left, 0, rows)
    pa = copies(block, block, partner)
    b.wait_recv()
    second = where(right, half, half)
    g = copies(second, second, p.in_plane(left))
    block = where(right, 0, rows)
    pb = copies(block, block, partner)
    yield
    f.wait_recv()
    g.wait_recv()
    block = where(far, 0, rows)
    pc = copies(block, block, partner)
    yield
    own.wait_recv()
    pa.wait_recv()
    pb.wait_recv()
    pc.wait_recv()


def whole(ref, rows):
    return lambda slot, offset, count: ref.at[at(slot, rows, offset, count)]


def column_ring(copies, p, src, ref):
    def block(distance):
        return ref.at[at(place(distance), TOK)]

    up, down = p.in_column(p.zslot(1)), p.in_column(p.zslot(-1))
    u = copies(src, block(-1), up)
    d = copies(src, block(1), down)
    for step in range(1, Z // 2 + 1):
        yield
        u.wait_recv()
        if step < Z // 2:
            u = copies(block(-step), block(-step - 1), up)
        if step < Z // 2:
            d.wait_recv()
            if step < Z // 2 - 1:
                d = copies(block(step), block(step + 1), down)


def run(*rings):
    rings = list(rings)
    while rings:
        rings = [ring for ring in rings if next(ring, True) is None]


def plane_peers(p):
    return [p.in_plane(p.xslot(s, f)) for s in range(X) for f in (False, True) if s or f]


def column_peers(p):
    return [p.in_column(p.zslot(s)) for s in range(1, Z)]


def row_peers(p):
    return [{"fsdp": p.yslot(s)} for s in range(1, Y)]


def sum_squares(ref, chunk=64):
    width = ref.shape[1]

    def step(i, acc):
        block = ref[pl.ds(pl.multiple_of(i * chunk, chunk), chunk), :].astype(F32)
        return acc + jnp.sum((block * block).reshape(chunk // 8, 8, width), axis=0)

    acc = lax.fori_loop(0, ref.shape[0] // chunk, step, jnp.zeros((8, width), F32))
    return jnp.sum(acc, axis=0, keepdims=True)


def place(distance):
    return (distance + Z - 2) % Z


def sum_squares(ref, chunk=64):
    width = ref.shape[1]

    def step(i, acc):
        block = ref[pl.ds(pl.multiple_of(i * chunk, chunk), chunk), :].astype(F32)
        return acc + jnp.sum((block * block).reshape(chunk // 8, 8, width), axis=0)

    acc = lax.fori_loop(0, ref.shape[0] // chunk, step, jnp.zeros((8, width), F32))
    return jnp.sum(acc, axis=0, keepdims=True)


def build_bias(owners, pos, bias, p):
    lane = lax.broadcasted_iota(jnp.int32, (1, TOK), 1)
    low = lane < HALF
    row = lax.broadcasted_iota(jnp.int32, (HALF, TOK), 0)

    def step(slot, carry):
        owner = owners[p.z * G + slot]
        where = lane + jnp.where(low, owner * HALF, (2 * PAIRS - 1 - owner) * HALF - HALF)
        floor = where - pos[slot, 0:1, :]
        cols = pl.ds(pl.multiple_of(slot * TOK, TOK), TOK)
        for distance in range(Z):
            owner = owners[p.zslot(distance) * G + p.slot]
            for h, stretch in enumerate((owner, 2 * PAIRS - 1 - owner)):
                key = row + stretch * HALF
                seen = (key <= where) & (key >= floor)
                rows = pl.ds(place(distance) * TOK + h * HALF, HALF)
                bias[rows, cols] = jnp.where(seen, 0.0, NEGATIVE)
        return carry

    lax.fori_loop(0, G, step, 0)


def tile_of(t):
    return pl.ds(pl.multiple_of(t * TILE, TILE), TILE)


def tile_stats(qg, dog, kg, vg, bias, out, t):
    tile = tile_of(t)
    for h in range(HEADS):
        cols = pl.ds(h * DH, DH)
        raw = lax.dot_general(kg[...], qg[tile, cols], LAST, preferred_element_type=F32)
        raw = raw + bias[:, tile]
        top = jnp.max(raw, axis=0, keepdims=True)
        mass = jnp.exp2((raw - top) * SCALE2)
        total = jnp.sum(mass, axis=0, keepdims=True)
        dp = lax.dot_general(vg[...], dog[tile, cols], LAST, preferred_element_type=F32)
        dsum = jnp.sum(mass * dp, axis=0, keepdims=True)
        out[h : h + 1, tile] = top * SCALE2 + jnp.log2(total)
        out[HEADS + h : HEADS + h + 1, tile] = dsum / total


def merge_stats(shared, merged):
    for h in range(HEADS):
        parts = shared[:, h, :]
        top = jnp.max(parts, axis=0, keepdims=True)
        weight = jnp.exp2(parts - top)
        total = jnp.sum(weight, axis=0, keepdims=True)
        merged[h : h + 1, :] = top + jnp.log2(total)
        dsum = jnp.sum(weight * shared[:, HEADS + h, :], axis=0, keepdims=True)
        merged[HEADS + h : HEADS + h + 1, :] = dsum / total


def half_grads(qg, dog, kg, vg, kt, bias, merged, probs, slopes, acc, dqt, dq, dk, dv, half):
    count = kg.shape[0] // 2
    rows = pl.ds(half * count, count)
    acc[...] = jnp.zeros_like(acc)

    def step(t, carry):
        tile = tile_of(t)
        for h in range(HEADS):
            cols = pl.ds(h * DH, DH)
            wide = pl.ds(h * TILE, TILE)
            raw = lax.dot_general(kg[rows, :], qg[tile, cols], LAST, preferred_element_type=F32)
            prob = jnp.exp2((raw + bias[rows, tile]) * SCALE2 - merged[h : h + 1, tile])
            dp = lax.dot_general(vg[rows, :], dog[tile, cols], LAST, preferred_element_type=F32)
            slope = prob * (dp - merged[HEADS + h : HEADS + h + 1, tile])
            probs[:, wide] = prob.astype(BF16)
            slopes[:, wide] = slope.astype(BF16)
            part = jnp.dot(kt[:, rows], slopes[:, wide], preferred_element_type=F32)
            if half == 0:
                dqt[t, :, wide] = part
            else:
                dq[tile, cols] = ((part + dqt[t, :, wide]) * SCALE).T.astype(BF16)
        tall = lambda ref: jnp.concatenate(
            [ref[tile, pl.ds(h * DH, DH)] for h in range(HEADS)], axis=0
        )
        acc[:, :DH] += jnp.dot(slopes[...], tall(qg), preferred_element_type=F32)
        acc[:, DH:] += jnp.dot(probs[...], tall(dog), preferred_element_type=F32)
        return carry

    lax.fori_loop(0, qg.shape[0] // TILE, step, 0)
    dk[rows, :] = (acc[:, :DH] * SCALE).astype(BF16)
    dv[rows, :] = acc[:, DH:].astype(BF16)


FARTHEST = (4, 3, 5, 2, 6, 1, 7)


def rounded_sum(ref, i, count):
    total = ref[i, 0].astype(F32)
    for n in range(1, count):
        total = total + ref[i, n].astype(F32)
    return total.astype(BF16)


def kernel(
    owners, q, do, k, v, pos, hid, kw, vw, dq_slots, raw_k, raw_v, sums,
    qg, dog, kg, vg, pg, bias, shared, merged, kt, probs, slopes, acc, dqt, dq, dk, dv,
    hg, hgt, pq, cq, gz, gy, grads, part, rz, ysum, wsum, tw,
    send, recv, share_send, share_recv, local,
):
    p = Place()
    group = lax.div(p.y * HEADS, HPG)
    head_cols = pl.ds(pl.multiple_of(group * DH, DH), DH)
    own_k, own_v = k.at[:, head_cols], v.at[:, head_cols]
    wide = hid.shape[1] // G
    piece = wide // Z
    mine = at(p.slot, TOK)
    members = Y // KVG

    def strip(slot):
        return hid.at[:, pl.ds(pl.multiple_of(slot * wide, 128), wide)]

    moves = [
        (q, qg.at[mine]),
        (do, dog.at[mine]),
        (own_k, kg.at[at(place(0), TOK)]),
        (own_v, vg.at[at(place(0), TOK)]),
        (strip(p.slot), hg.at[mine]),
        (kw, tw.at[0]),
        (vw, tw.at[1]),
    ]
    loads = [pltpu.make_async_copy(s, d, local.at[i]) for i, (s, d) in enumerate(moves)]
    for load in loads:
        load.start()
    pg[p.slot] = jnp.broadcast_to(pos[...], (8, TOK))
    barrier(plane_peers(p) + column_peers(p) + row_peers(p))
    copies = Copies(send, recv)
    small = [copies(pg.at[p.slot], pg.at[p.slot], peer) for peer in plane_peers(p)]
    kr = column_ring(copies, p, own_k, kg)
    vr = column_ring(copies, p, own_v, vg)
    qr = plane_ring(copies, p, q, whole(qg, TOK), TOK)
    dr = plane_ring(copies, p, do, whole(dog, TOK), TOK)
    for ring in (kr, vr, qr, dr):
        next(ring)
    for ring in (kr, vr):
        next(ring)
    for copy in small:
        copy.wait_recv()
    build_bias(owners, pg, bias, p)
    for ring in (kr, vr, qr):
        next(ring)
    for i in range(2):
        loads[5 + i].wait()
        wsum[i] = jnp.broadcast_to(sum_squares(tw.at[i]), wsum.shape[1:])
    for ring in (kr, vr, dr, qr, kr, vr, dr):
        next(ring, None)
    hs = []
    for s, f in ((2, False), (2, True), (1, False), (3, False), (1, True), (3, True), (0, True)):
        to = p.xslot(s, f)
        hs.append(copies(strip(to), hg.at[mine], p.in_plane(to)))
    run(qr, dr)
    for load in loads[:5]:
        load.wait()
    kt[...] = kg[...].T
    peers = plane_peers(p)
    mine_stats = shared.at[p.slot]

    def share(t):
        block = shared.at[p.slot, :, tile_of(t)]
        return [
            pltpu.make_async_remote_copy(
                src_ref=block,
                dst_ref=block,
                send_sem=share_send.at[n, t],
                recv_sem=share_recv.at[n, t],
                device_id=peer,
                device_id_type=MESH,
            )
            for n, peer in enumerate(peers)
        ]

    def stats_step(t, carry):
        tile_stats(qg, dog, kg, vg, bias, mine_stats, t)
        for copy in share(t):
            copy.start()
        return carry

    tiles = qg.shape[0] // TILE
    lax.fori_loop(0, tiles, stats_step, 0)
    for t in range(tiles):
        for copy in share(t):
            copy.wait_recv()
            copy.wait_send()
    merge_stats(shared, merged)

    def scatter(half):
        near = {0: (4, 3, 5, 2), 1: (6, 1, 7)}[half]
        return [
            [
                copies(src.at[at(place(s), TOK)], gz.at[i, p.z], p.in_column(p.zslot(s)))
                for s in near
            ]
            for i, src in enumerate((dk, dv))
        ]

    halves = []
    for half in range(2):
        half_grads(
            qg, dog, kg, vg, kt, bias, merged, probs, slopes, acc, dqt, dq, dk, dv, half
        )
        halves.append(scatter(half))
    own_g = [
        pltpu.make_async_copy(src.at[at(place(0), TOK)], gz.at[i, p.z], local.at[7 + i])
        for i, src in enumerate((dk, dv))
    ]
    for load in own_g:
        load.start()

    def stream(i, raw):
        made = halves[0][i] + halves[1][i]
        own_g[i].wait()
        for copy in made:
            copy.wait_recv()
        gy[i, p.y] = rounded_sum(gz, i, Z)
        made = [copies(gy.at[i, p.y], gy.at[i, p.y], peer) for peer in row_peers(p)]
        yield
        for copy in made:
            copy.wait_recv()
        for g in range(KVG):
            total = gy[i, g * members].astype(F32)
            for n in range(1, members):
                total = total + gy[i, g * members + n].astype(F32)
            grads[i, mine, g * DH : (g + 1) * DH] = total.astype(BF16)
        ring = plane_ring(copies, p, grads.at[i, mine], whole(grads.at[i], TOK), TOK)
        for _ in ring:
            yield
        product = jnp.dot(hgt[...], grads[i], preferred_element_type=F32)
        part[i] = product.astype(BF16)
        rz[i, p.z] = part[i, at(p.z, piece), :]
        made = [
            copies(part.at[i, at(p.zslot(s), piece)], rz.at[i, p.z], p.in_column(p.zslot(s)))
            for s in FARTHEST
        ]
        yield
        for copy in made:
            copy.wait_recv()
        own = pl.ds(pl.multiple_of(p.slot * wide + p.z * piece, 16), piece)
        raw[own, :] = rounded_sum(rz, i, Z)
        made = [
            copies(raw.at[own], raw.at[own], p.in_column(p.zslot(s))) for s in FARTHEST
        ]
        yield
        for copy in made:
            copy.wait_recv()
        ring = plane_ring(copies, p, raw.at[at(p.slot, wide)], whole(raw, wide), wide)
        next(ring)
        square = sum_squares(raw.at[at(p.slot, wide)])
        row = lax.broadcasted_iota(jnp.int32, (8, square.shape[1]), 0)
        ysum[i, p.y] = jnp.where(row == 0, square, wsum[i])
        made = [copies(ysum.at[i, p.y], ysum.at[i, p.y], peer) for peer in row_peers(p)]
        yield
        next(ring)
        for copy in made:
            copy.wait_recv()
        total = ysum[i, 0]
        for n in range(1, Y):
            total = total + ysum[i, n]
        sums[i, p.slot] = total
        made = [copies(sums.at[i, p.slot], sums.at[i, p.slot], peer) for peer in plane_peers(p)]
        yield
        next(ring)
        yield
        for _ in ring:
            pass
        for copy in made:
            copy.wait_recv()

    partner = p.in_plane(p.xslot(0, True))
    given = [copies(dq.at[at(x * C + 1 - p.c, TOK)], pq.at[x], partner) for x in range(X)]
    for copy in hs:
        copy.wait_recv()
    hgt[...] = hg[...].T
    streams = [stream(0, raw_k), stream(1, raw_v)]
    for one in streams:
        next(one)
    for x in range(X):
        given[x].wait_recv()
        cq[x] = (dq[at(x * C + p.c, TOK), :].astype(F32) + pq[x].astype(F32)).astype(BF16)
    qs = []
    for s in (2, 1, 3):
        to = lax.rem(p.x + s, X)
        qs.append(copies(cq.at[to], dq_slots.at[p.x], p.in_plane(to * C + p.c)))
    dq_slots[p.x] = cq[p.x]
    run(*streams)
    for copy in qs:
        copy.wait_recv()
    copies.wait_sends()


def shape(dims, kind=BF16):
    return jax.ShapeDtypeStruct(dims, kind)


def dma(n):
    return pltpu.SemaphoreType.DMA((n,))


def local(
    queries, keys, values, out_grad, hidden, key_weight, value_weight, stretch_owner, positions
):
    width = queries.shape[1]
    model = hidden.shape[1]
    piece = model // G
    columns = KVG * DH
    dq_slots, raw_k, raw_v, sums = pl.pallas_call(
        kernel,
        out_shape=(
            shape((X, TOK, width)),
            shape((model, columns)),
            shape((model, columns)),
            shape((2, G, 8, columns), F32),
        ),
        in_specs=[SMEM] + [ANY] * 4 + [VMEM] + [ANY] * 3,
        out_specs=(VMEM,) * 4,
        scratch_shapes=[
            pltpu.VMEM((ROWS, width), BF16),
            pltpu.VMEM((ROWS, width), BF16),
            pltpu.VMEM((Z * TOK, DH), BF16),
            pltpu.VMEM((Z * TOK, DH), BF16),
            pltpu.VMEM((G, 8, TOK), jnp.int32),
            pltpu.VMEM((Z * TOK, ROWS), F32),
            pltpu.VMEM((G, 2 * HEADS, ROWS), F32),
            pltpu.VMEM((2 * HEADS, ROWS), F32),
            pltpu.VMEM((DH, Z * TOK), BF16),
            pltpu.VMEM((Z * TOK // 2, HEADS * TILE), BF16),
            pltpu.VMEM((Z * TOK // 2, HEADS * TILE), BF16),
            pltpu.VMEM((Z * TOK // 2, 2 * DH), F32),
            pltpu.VMEM((ROWS // TILE, DH, HEADS * TILE), F32),
            pltpu.VMEM((ROWS, width), BF16),
            pltpu.VMEM((Z * TOK, DH), BF16),
            pltpu.VMEM((Z * TOK, DH), BF16),
            pltpu.VMEM((ROWS, piece), BF16),
            pltpu.VMEM((piece, ROWS), BF16),
            pltpu.VMEM((X, TOK, width), BF16),
            pltpu.VMEM((X, TOK, width), BF16),
            pltpu.VMEM((2, Z, TOK, DH), BF16),
            pltpu.VMEM((2, Y, TOK, DH), BF16),
            pltpu.VMEM((2, ROWS, columns), BF16),
            pltpu.VMEM((2, piece, columns), BF16),
            pltpu.VMEM((2, Z, piece // Z, columns), BF16),
            pltpu.VMEM((2, Y, 8, columns), F32),
            pltpu.VMEM((2, 8, columns), F32),
            pltpu.VMEM((2, model, columns), BF16),
            dma(180),
            dma(180),
            pltpu.SemaphoreType.DMA((G - 1, ROWS // TILE)),
            pltpu.SemaphoreType.DMA((G - 1, ROWS // TILE)),
            dma(9),
        ],
        compiler_params=pltpu.CompilerParams(
            collective_id=0, has_side_effects=True, vmem_limit_bytes=VMEM_BYTES
        ),
    )(
        stretch_owner, queries, out_grad, keys, values, positions.reshape(1, TOK),
        hidden, key_weight, value_weight,
    )
    query_grad = jnp.sum(dq_slots.astype(F32), axis=0).astype(BF16)
    tokens = TOK * PAIRS

    def clipped(i, raw):
        grad_norm = jnp.sqrt(jnp.sum(sums[i, :, 0], axis=0) + EPSILON)
        weight_norm = jnp.sqrt(sums[i, 0, 1] + EPSILON)
        factor = jnp.minimum(1.0, CLIP_RATE * tokens * weight_norm / grad_norm)
        return raw.astype(F32) * factor[None, :]

    return (query_grad, clipped(0, raw_k), clipped(1, raw_v))


def solution(mesh):
    return jax.shard_map(
        local,
        mesh=mesh,
        in_specs=(
            P("ctx", "fsdp"),
            P("ctx", None),
            P("ctx", None),
            P("ctx", "fsdp"),
            P("ctx", "fsdp"),
            P("fsdp", None),
            P("fsdp", None),
            P(),
            P("ctx"),
        ),
        out_specs=(P("ctx", "fsdp"), P("fsdp", None), P("fsdp", None)),
        check_vma=False,
    )
```

time: 122 us -> 116 us (0.951)
  Pallas kernels: 113 us -> 107 us
  local copies, waits for them, and re-layouts: 4.82 us -> 0 us
  other arithmetic: 3.15 us -> 7.33 us
    pallas_call x5 -> x1, Pallas kernels: 113 us -> 107 us  [local(): pl.pallas_call(kernel, out_shape=(shape((X, TOK, width)), shape((model, c...]
    unnamed x20 -> x0, local copies, waits for them, and re-layouts: 4.82 us -> none
    mul x1, other arithmetic: 2.35 us -> 3.89 us  [clipped(): return raw.astype(F32) * factor[None, :]]
where the time goes in v4:
time: 116 us; the launch traced here: 115 us
  Pallas kernels  107 us (92%)
  other arithmetic  7.33 us (6%)
    pallas_call x1, Pallas kernels, local(): pl.pallas_call(kernel, out_shape=(shape((X, TOK, width)), shape((model, c...  107 us
    mul x1, other arithmetic, clipped(): return raw.astype(F32) * factor[None, :]  3.89 us

profile of v4, /device:TPU:1, one launch (start us, length us, event | category | flops | bytes accessed | tf_op | source)
XLA Modules:
  0.0 115.1 jit_solution(2346262912603350978)
XLA Ops:
  0.6 107.1 %shard_map.112 = (bf16[4,128,512]{2,1,0:T(8,128)(2,1)}, bf16[2048,256]{1,0:T(8,128)(2,1)}, bf16[2048,256]{1,0:T(8,128)(2,1)}, f32[2,8,8,256]{3,2,1,0:T(8,128)}) custom-call(s32[64]{0:T(128)} %owners.1, bf16[128,512]{1,0:T(8,128)(2,1)} %q.1, bf16[128,512]{1,0:T(8,128)(2,1)} %do.1, bf16[128,256]{1,0:T(8,128)(2,1)} %k.1, bf16[128,256]{1,0:T(8,128)(2,1)} %v.1, ...), custom_call_target="tpu_custom_call" | custom-call | tf_op jit(solution)/shard_map/pallas_call | solution.py:506
  107.7 1.8 %reduce_sum.30 = bf16[128,512]{1,0:T(8,128)(2,1)} reduce(bf16[4,128,512]{2,1,0:T(8,128)(2,1)} %get-tuple-element.7, bf16[]{:T(256)} %constant.1.clone.1), dimensions={0}, to_apply=%region_0.0 | reduce | flops 196608 | bytes 655362 | tf_op jit(solution)/shard_map/reduce_sum | solution.py:558
  109.5 0.9 slice_reduce_fusion
  110.4 0.7 sqrt_multiply_fusion
  111.2 3.9 %convert_multiply_fusion = (f32[2048,256]{1,0:T(8,128)}, f32[2048,256]{1,0:T(8,128)}) fusion(bf16[2048,256]{1,0:T(8,128)(2,1)} %get-tuple-element.10, f32[256]{0:T(256)S(1)} %multiply_minimum_fusion, f32[256]{0:T(256)S(1)} %multiply_minimum_fusion.1, bf16[2048,256]{1,0:T(8,128)(2,1)} %get-tuple-element.8), kind=kLoop, calls=%fused_computation | loop fusion | flops 2097152 | bytes 6293504 | tf_op jit(solution)/shard_map/mul | solution.py:565
  (2 shorter events, 0.0 us)

commit v5 on v4

--- a/solution.py
+++ b/solution.py
@@ -23,7 +23,8 @@
 ROWS = G * TOK
 CLIP_RATE = 0.02
 TILE = 256
-VMEM_BYTES = 62 * 1024 * 1024
+VMEM_BYTES = 55 * 1024 * 1024
+CHUNKS = 2
 EPSILON = 1e-06
 NEGATIVE = -1e30
 SCALE = 1.0 / math.sqrt(DH)
@@ -89,11 +90,15 @@
             copy.wait_send()
 
 
-def barrier(devices):
-    sem = pltpu.get_barrier_semaphore()
+def greet(devices):
     for device in devices:
-        pl.semaphore_signal(sem, inc=1, device_id=device, device_id_type=MESH)
-    pl.semaphore_wait(sem, len(devices))
+        pl.semaphore_signal(
+            pltpu.get_barrier_semaphore(), inc=1, device_id=device, device_id_type=MESH
+        )
+
+
+def meet(devices):
+    pl.semaphore_wait(pltpu.get_barrier_semaphore(), len(devices))
 
 
 def at(slot, rows, offset=0, count=None):
@@ -224,7 +229,11 @@
     return pl.ds(pl.multiple_of(t * TILE, TILE), TILE)
 
 
-def tile_stats(qg, dog, kg, vg, bias, out, t):
+def head_of(t, h):
+    return pl.ds(pl.multiple_of((t * HEADS + h) * TILE, TILE), TILE)
+
+
+def tile_stats(qg, dog, kg, vg, bias, masses, dps, tops, out, t):
     tile = tile_of(t)
     for h in range(HEADS):
         cols = pl.ds(h * DH, DH)
@@ -233,44 +242,51 @@
         top = jnp.max(raw, axis=0, keepdims=True)
         mass = jnp.exp2((raw - top) * SCALE2)
         total = jnp.sum(mass, axis=0, keepdims=True)
+        masses[:, head_of(t, h)] = mass.astype(BF16)
         dp = lax.dot_general(vg[...], dog[tile, cols], LAST, preferred_element_type=F32)
+        dps[:, head_of(t, h)] = dp
         dsum = jnp.sum(mass * dp, axis=0, keepdims=True)
+        tops[h : h + 1, tile] = top * SCALE2
         out[h : h + 1, tile] = top * SCALE2 + jnp.log2(total)
         out[HEADS + h : HEADS + h + 1, tile] = dsum / total
 
 
-def merge_stats(shared, merged):
+def merge_stats(shared, tops, merged, t):
+    tile = tile_of(t)
     for h in range(HEADS):
-        parts = shared[:, h, :]
+        parts = shared[:, h, tile]
         top = jnp.max(parts, axis=0, keepdims=True)
         weight = jnp.exp2(parts - top)
         total = jnp.sum(weight, axis=0, keepdims=True)
-        merged[h : h + 1, :] = top + jnp.log2(total)
-        dsum = jnp.sum(weight * shared[:, HEADS + h, :], axis=0, keepdims=True)
-        merged[HEADS + h : HEADS + h + 1, :] = dsum / total
-
-
-def half_grads(qg, dog, kg, vg, kt, bias, merged, probs, slopes, acc, dqt, dq, dk, dv, half):
-    count = kg.shape[0] // 2
-    rows = pl.ds(half * count, count)
+        merged[h : h + 1, tile] = jnp.exp2(tops[h : h + 1, tile] - (top + jnp.log2(total)))
+        dsum = jnp.sum(weight * shared[:, HEADS + h, tile], axis=0, keepdims=True)
+        merged[HEADS + h : HEADS + h + 1, tile] = dsum / total
+
+
+def chunk_grads(
+    qg, dog, kt, masses, dps, merged, probs, slopes, acc, dqt, dq, dk, dv, chunk, ready
+):
+    count = masses.shape[0] // CHUNKS
+    rows = pl.ds(chunk * count, count)
     acc[...] = jnp.zeros_like(acc)
 
     def step(t, carry):
+        ready(t)
         tile = tile_of(t)
         for h in range(HEADS):
             cols = pl.ds(h * DH, DH)
             wide = pl.ds(h * TILE, TILE)
-            raw = lax.dot_general(kg[rows, :], qg[tile, cols], LAST, preferred_element_type=F32)
-            prob = jnp.exp2((raw + bias[rows, tile]) * SCALE2 - merged[h : h + 1, tile])
-            dp = lax.dot_general(vg[rows, :], dog[tile, cols], LAST, preferred_element_type=F32)
-            slope = prob * (dp - merged[HEADS + h : HEADS + h + 1, tile])
+            prob = masses[rows, head_of(t, h)].astype(F32) * merged[h : h + 1, tile]
+            slope = prob * (dps[rows, head_of(t, h)] - merged[HEADS + h : HEADS + h + 1, tile])
             probs[:, wide] = prob.astype(BF16)
             slopes[:, wide] = slope.astype(BF16)
             part = jnp.dot(kt[:, rows], slopes[:, wide], preferred_element_type=F32)
-            if half == 0:
+            if chunk > 0:
+                part = part + dqt[t, :, wide]
+            if chunk < CHUNKS - 1:
                 dqt[t, :, wide] = part
             else:
-                dq[tile, cols] = ((part + dqt[t, :, wide]) * SCALE).T.astype(BF16)
+                dq[tile, cols] = (part * SCALE).T.astype(BF16)
         tall = lambda ref: jnp.concatenate(
             [ref[tile, pl.ds(h * DH, DH)] for h in range(HEADS)], axis=0
         )
@@ -295,7 +311,7 @@
 
 def kernel(
     owners, q, do, k, v, pos, hid, kw, vw, dq_slots, raw_k, raw_v, sums,
-    qg, dog, kg, vg, pg, bias, shared, merged, kt, probs, slopes, acc, dqt, dq, dk, dv,
+    qg, dog, kg, vg, pg, bias, shared, merged, kt, masses, dps, tops, probs, slopes, acc, dqt, dq, dk, dv,
     hg, hgt, pq, cq, gz, gy, grads, part, rz, ysum, wsum, tw,
     send, recv, share_send, share_recv, local,
 ):
@@ -320,11 +336,16 @@
         (kw, tw.at[0]),
         (vw, tw.at[1]),
     ]
+    everyone = plane_peers(p) + column_peers(p) + row_peers(p)
+    greet(everyone)
     loads = [pltpu.make_async_copy(s, d, local.at[i]) for i, (s, d) in enumerate(moves)]
-    for load in loads:
+    for load in loads[5:] + loads[:5]:
         load.start()
     pg[p.slot] = jnp.broadcast_to(pos[...], (8, TOK))
-    barrier(plane_peers(p) + column_peers(p) + row_peers(p))
+    for i in range(2):
+        loads[5 + i].wait()
+        wsum[i] = jnp.broadcast_to(sum_squares(tw.at[i]), wsum.shape[1:])
+    meet(everyone)
     copies = Copies(send, recv)
     small = [copies(pg.at[p.slot], pg.at[p.slot], peer) for peer in plane_peers(p)]
     kr = column_ring(copies, p, own_k, kg)
@@ -340,16 +361,13 @@
     build_bias(owners, pg, bias, p)
     for ring in (kr, vr, qr):
         next(ring)
-    for i in range(2):
-        loads[5 + i].wait()
-        wsum[i] = jnp.broadcast_to(sum_squares(tw.at[i]), wsum.shape[1:])
     for ring in (kr, vr, dr, qr, kr, vr, dr):
         next(ring, None)
+    run(qr, dr)
     hs = []
     for s, f in ((2, False), (2, True), (1, False), (3, False), (1, True), (3, True), (0, True)):
         to = p.xslot(s, f)
         hs.append(copies(strip(to), hg.at[mine], p.in_plane(to)))
-    run(qr, dr)
     for load in loads[:5]:
         load.wait()
     kt[...] = kg[...].T
@@ -371,21 +389,22 @@
         ]
 
     def stats_step(t, carry):
-        tile_stats(qg, dog, kg, vg, bias, mine_stats, t)
+        tile_stats(qg, dog, kg, vg, bias, masses, dps, tops, mine_stats, t)
         for copy in share(t):
             copy.start()
         return carry
 
     tiles = qg.shape[0] // TILE
     lax.fori_loop(0, tiles, stats_step, 0)
-    for t in range(tiles):
+
+    def ready(t):
         for copy in share(t):
             copy.wait_recv()
-            copy.wait_send()
-    merge_stats(shared, merged)
-
-    def scatter(half):
-        near = {0: (4, 3, 5, 2), 1: (6, 1, 7)}[half]
+        merge_stats(shared, tops, merged, t)
+
+    def scatter(chunk):
+        count = Z // CHUNKS
+        near = [s for s in FARTHEST if place(s) // count == chunk]
         return [
             [
                 copies(src.at[at(place(s), TOK)], gz.at[i, p.z], p.in_column(p.zslot(s)))
@@ -394,12 +413,13 @@
             for i, src in enumerate((dk, dv))
         ]
 
-    halves = []
-    for half in range(2):
-        half_grads(
-            qg, dog, kg, vg, kt, bias, merged, probs, slopes, acc, dqt, dq, dk, dv, half
+    chunks = []
+    for chunk in range(CHUNKS):
+        chunk_grads(
+            qg, dog, kt, masses, dps, merged, probs, slopes, acc, dqt, dq, dk, dv, chunk,
+            ready if chunk == 0 else lambda t: None,
         )
-        halves.append(scatter(half))
+        chunks.append(scatter(chunk))
     own_g = [
         pltpu.make_async_copy(src.at[at(place(0), TOK)], gz.at[i, p.z], local.at[7 + i])
         for i, src in enumerate((dk, dv))
@@ -408,7 +428,7 @@
         load.start()
 
     def stream(i, raw):
-        made = halves[0][i] + halves[1][i]
+        made = [copy for parts in chunks for copy in parts[i]]
         own_g[i].wait()
         for copy in made:
             copy.wait_recv()
@@ -486,6 +506,9 @@
     for copy in qs:
         copy.wait_recv()
     copies.wait_sends()
+    for t in range(tiles):
+        for copy in share(t):
+            copy.wait_send()
 
 
 def shape(dims, kind=BF16):
@@ -506,10 +529,10 @@
     dq_slots, raw_k, raw_v, sums = pl.pallas_call(
         kernel,
         out_shape=(
-            shape((X, TOK, width)),
-            shape((model, columns)),
-            shape((model, columns)),
-            shape((2, G, 8, columns), F32),
+            pltpu.VMEM((X, TOK, width), BF16),
+            pltpu.VMEM((model, columns), BF16),
+            pltpu.VMEM((model, columns), BF16),
+            pltpu.VMEM((2, G, 8, columns), F32),
         ),
         in_specs=[SMEM] + [ANY] * 4 + [VMEM] + [ANY] * 3,
         out_specs=(VMEM,) * 4,
@@ -523,9 +546,12 @@
             pltpu.VMEM((G, 2 * HEADS, ROWS), F32),
             pltpu.VMEM((2 * HEADS, ROWS), F32),
             pltpu.VMEM((DH, Z * TOK), BF16),
-            pltpu.VMEM((Z * TOK // 2, HEADS * TILE), BF16),
-            pltpu.VMEM((Z * TOK // 2, HEADS * TILE), BF16),
-            pltpu.VMEM((Z * TOK // 2, 2 * DH), F32),
+            pltpu.VMEM((Z * TOK, HEADS * ROWS), BF16),
+            pltpu.VMEM((Z * TOK, HEADS * ROWS), F32),
+            pltpu.VMEM((8, ROWS), F32),
+            pltpu.VMEM((Z * TOK // CHUNKS, HEADS * TILE), BF16),
+            pltpu.VMEM((Z * TOK // CHUNKS, HEADS * TILE), BF16),
+            pltpu.VMEM((Z * TOK // CHUNKS, 2 * DH), F32),
             pltpu.VMEM((ROWS // TILE, DH, HEADS * TILE), F32),
             pltpu.VMEM((ROWS, width), BF16),
             pltpu.VMEM((Z * TOK, DH), BF16),

time: 116 us -> 104 us (0.90)
  Pallas kernels: 107 us -> 99.8 us
  other arithmetic: 7.33 us -> 3.15 us
    pallas_call x1, Pallas kernels: 107 us -> 99.8 us  [local(): pl.pallas_call(kernel, out_shape=(pltpu.VMEM((X, TOK, width), BF16), pltp...]
    mul x1, other arithmetic: 3.89 us -> 2.35 us  [clipped(): return raw.astype(F32) * factor[None, :]]
where the time goes in v5:
time: 104 us
  Pallas kernels  99.8 us (96%)
  other arithmetic  3.15 us (3%)
    pallas_call x1, Pallas kernels, local(): pl.pallas_call(kernel, out_shape=(pltpu.VMEM((X, TOK, width), BF16), pltp...  99.8 us
    mul x1, other arithmetic, clipped(): return raw.astype(F32) * factor[None, :]  2.35 us

profile of v5, /device:TPU:1, one launch (start us, length us, event | category | flops | bytes accessed | tf_op | source)
XLA Modules:
  0.0 103.6 jit_solution(16623237032169228800)
XLA Ops:
  0.6 99.8 %shard_map.112 = (bf16[4,128,512]{2,1,0:T(8,128)(2,1)S(1)}, bf16[2048,256]{1,0:T(8,128)(2,1)S(1)}, bf16[2048,256]{1,0:T(8,128)(2,1)S(1)}, f32[2,8,8,256]{3,2,1,0:T(8,128)S(1)}) custom-call(s32[64]{0:T(128)} %owners.1, bf16[128,512]{1,0:T(8,128)(2,1)} %q.1, bf16[128,512]{1,0:T(8,128)(2,1)} %do.1, bf16[128,256]{1,0:T(8,128)(2,1)} %k.1, bf16[128,256]{1,0:T(8,128)(2,1)} %v.1, ...), custom_call_target="tpu_custom_call" | custom-call | tf_op jit(solution)/shard_map/pallas_call | solution.py:529
  100.4 0.7 reduce_sum.30
  101.3 2.3 %convert_multiply_fusion = (f32[2048,256]{1,0:T(8,128)}, f32[2048,256]{1,0:T(8,128)}) fusion(bf16[2048,256]{1,0:T(8,128)(2,1)S(1)} %get-tuple-element.10, f32[256]{0:T(256)S(1)} %multiply_minimum_fusion, f32[256]{0:T(256)S(1)} %multiply_minimum_fusion.1, bf16[2048,256]{1,0:T(8,128)(2,1)S(1)} %get-tuple-element.8), kind=kLoop, calls=%fused_computation | loop fusion | flops 2097152 | bytes 6293504 | tf_op jit(solution)/shard_map/mul | solution.py:591
  (4 shorter events, 0.1 us)

commit v6 on v5

--- a/solution.py
+++ b/solution.py
@@ -24,7 +24,8 @@
 CLIP_RATE = 0.02
 TILE = 256
 VMEM_BYTES = 55 * 1024 * 1024
-CHUNKS = 2
+CHUNKS = 4
+ORDER = (3, 5, 4, 2, 6, 1, 7, 0)
 EPSILON = 1e-06
 NEGATIVE = -1e30
 SCALE = 1.0 / math.sqrt(DH)
@@ -137,6 +138,25 @@
     pc.wait_recv()
 
 
+def plane_direct(copies, p, src, where, rows):
+    partner = p.in_plane(p.xslot(0, True))
+    mine = where(p.slot, 0, rows)
+    c, a, b = [copies(src, mine, p.in_plane(p.xslot(s))) for s in (2, 1, -1)]
+    passed = [copies(src, mine, partner)]
+    yield
+    for copy, s in ((a, -1), (b, 1)):
+        copy.wait_recv()
+        block = where(p.xslot(s), 0, rows)
+        passed.append(copies(block, block, partner))
+    yield
+    c.wait_recv()
+    block = where(p.xslot(2), 0, rows)
+    passed.append(copies(block, block, partner))
+    yield
+    for copy in passed:
+        copy.wait_recv()
+
+
 def whole(ref, rows):
     return lambda slot, offset, count: ref.at[at(slot, rows, offset, count)]
 
@@ -189,7 +209,7 @@
 
 
 def place(distance):
-    return (distance + Z - 2) % Z
+    return ORDER.index(distance % Z)
 
 
 def sum_squares(ref, chunk=64):
@@ -312,7 +332,7 @@
 def kernel(
     owners, q, do, k, v, pos, hid, kw, vw, dq_slots, raw_k, raw_v, sums,
     qg, dog, kg, vg, pg, bias, shared, merged, kt, masses, dps, tops, probs, slopes, acc, dqt, dq, dk, dv,
-    hg, hgt, pq, cq, gz, gy, grads, part, rz, ysum, wsum, tw,
+    hg, hgt, pq, cq, gz, gy, grads, part, rz, ysum, wsum, tw, block, tot,
     send, recv, share_send, share_recv, local,
 ):
     p = Place()
@@ -350,8 +370,8 @@
     small = [copies(pg.at[p.slot], pg.at[p.slot], peer) for peer in plane_peers(p)]
     kr = column_ring(copies, p, own_k, kg)
     vr = column_ring(copies, p, own_v, vg)
-    qr = plane_ring(copies, p, q, whole(qg, TOK), TOK)
-    dr = plane_ring(copies, p, do, whole(dog, TOK), TOK)
+    qr = plane_direct(copies, p, q, whole(qg, TOK), TOK)
+    dr = plane_direct(copies, p, do, whole(dog, TOK), TOK)
     for ring in (kr, vr, qr, dr):
         next(ring)
     for ring in (kr, vr):
@@ -361,7 +381,7 @@
     build_bias(owners, pg, bias, p)
     for ring in (kr, vr, qr):
         next(ring)
-    for ring in (kr, vr, dr, qr, kr, vr, dr):
+    for ring in (kr, vr, dr, kr, vr, qr, dr):
         next(ring, None)
     run(qr, dr)
     hs = []
@@ -442,7 +462,7 @@
             for n in range(1, members):
                 total = total + gy[i, g * members + n].astype(F32)
             grads[i, mine, g * DH : (g + 1) * DH] = total.astype(BF16)
-        ring = plane_ring(copies, p, grads.at[i, mine], whole(grads.at[i], TOK), TOK)
+        ring = plane_direct(copies, p, grads.at[i, mine], whole(grads.at[i], TOK), TOK)
         for _ in ring:
             yield
         product = jnp.dot(hgt[...], grads[i], preferred_element_type=F32)
@@ -455,17 +475,23 @@
         yield
         for copy in made:
             copy.wait_recv()
-        own = pl.ds(pl.multiple_of(p.slot * wide + p.z * piece, 16), piece)
-        raw[own, :] = rounded_sum(rz, i, Z)
+        own = at(p.z, piece)
+        block[i, own, :] = rounded_sum(rz, i, Z)
         made = [
-            copies(raw.at[own], raw.at[own], p.in_column(p.zslot(s))) for s in FARTHEST
+            copies(block.at[i, own], block.at[i, own], p.in_column(p.zslot(s)))
+            for s in FARTHEST
         ]
         yield
         for copy in made:
             copy.wait_recv()
-        ring = plane_ring(copies, p, raw.at[at(p.slot, wide)], whole(raw, wide), wide)
+        ring = plane_ring(copies, p, block.at[i], whole(raw, wide), wide)
         next(ring)
-        square = sum_squares(raw.at[at(p.slot, wide)])
+        puts = [
+            pltpu.make_async_copy(block.at[i], raw.at[at(p.slot, wide)], local.at[9 + i]),
+            pltpu.make_async_copy(tot.at[i], sums.at[i, p.slot], local.at[11 + i]),
+        ]
+        puts[0].start()
+        square = sum_squares(block.at[i])
         row = lax.broadcasted_iota(jnp.int32, (8, square.shape[1]), 0)
         ysum[i, p.y] = jnp.where(row == 0, square, wsum[i])
         made = [copies(ysum.at[i, p.y], ysum.at[i, p.y], peer) for peer in row_peers(p)]
@@ -476,8 +502,9 @@
         total = ysum[i, 0]
         for n in range(1, Y):
             total = total + ysum[i, n]
-        sums[i, p.slot] = total
-        made = [copies(sums.at[i, p.slot], sums.at[i, p.slot], peer) for peer in plane_peers(p)]
+        tot[i] = total
+        puts[1].start()
+        made = [copies(tot.at[i], sums.at[i, p.slot], peer) for peer in plane_peers(p)]
         yield
         next(ring)
         yield
@@ -485,6 +512,8 @@
             pass
         for copy in made:
             copy.wait_recv()
+        for put in puts:
+            put.wait()
 
     partner = p.in_plane(p.xslot(0, True))
     given = [copies(dq.at[at(x * C + 1 - p.c, TOK)], pq.at[x], partner) for x in range(X)]
@@ -501,10 +530,12 @@
     for s in (2, 1, 3):
         to = lax.rem(p.x + s, X)
         qs.append(copies(cq.at[to], dq_slots.at[p.x], p.in_plane(to * C + p.c)))
-    dq_slots[p.x] = cq[p.x]
+    put_q = pltpu.make_async_copy(cq.at[p.x], dq_slots.at[p.x], local.at[13])
+    put_q.start()
     run(*streams)
     for copy in qs:
         copy.wait_recv()
+    put_q.wait()
     copies.wait_sends()
     for t in range(tiles):
         for copy in share(t):
@@ -535,7 +566,7 @@
             pltpu.VMEM((2, G, 8, columns), F32),
         ),
         in_specs=[SMEM] + [ANY] * 4 + [VMEM] + [ANY] * 3,
-        out_specs=(VMEM,) * 4,
+        out_specs=(ANY,) * 4,
         scratch_shapes=[
             pltpu.VMEM((ROWS, width), BF16),
             pltpu.VMEM((ROWS, width), BF16),
@@ -568,11 +599,13 @@
             pltpu.VMEM((2, Y, 8, columns), F32),
             pltpu.VMEM((2, 8, columns), F32),
             pltpu.VMEM((2, model, columns), BF16),
+            pltpu.VMEM((2, piece, columns), BF16),
+            pltpu.VMEM((2, 8, columns), F32),
             dma(180),
             dma(180),
             pltpu.SemaphoreType.DMA((G - 1, ROWS // TILE)),
             pltpu.SemaphoreType.DMA((G - 1, ROWS // TILE)),
-            dma(9),
+            dma(14),
         ],
         compiler_params=pltpu.CompilerParams(
             collective_id=0, has_side_effects=True, vmem_limit_bytes=VMEM_BYTES

time: 104 us -> 102 us (0.981)
  Pallas kernels: 99.8 us -> 98.2 us
    pallas_call x1, Pallas kernels: 99.8 us -> 98.2 us  [local(): pl.pallas_call(kernel, out_shape=(pltpu.VMEM((X, TOK, width), BF16), pltp...]
where the time goes in v6:
time: 102 us
  Pallas kernels  98.2 us (96%)
  other arithmetic  3.15 us (3%)
    pallas_call x1, Pallas kernels, local(): pl.pallas_call(kernel, out_shape=(pltpu.VMEM((X, TOK, width), BF16), pltp...  98.2 us
    mul x1, other arithmetic, clipped(): return raw.astype(F32) * factor[None, :]  2.35 us

profile of v6, /device:TPU:1, one launch (start us, length us, event | category | flops | bytes accessed | tf_op | source)
XLA Modules:
  0.0 102.0 jit_solution(5071877925211877840)
XLA Ops:
  0.6 98.2 %shard_map.112 = (bf16[4,128,512]{2,1,0:T(8,128)(2,1)S(1)}, bf16[2048,256]{1,0:T(8,128)(2,1)S(1)}, bf16[2048,256]{1,0:T(8,128)(2,1)S(1)}, f32[2,8,8,256]{3,2,1,0:T(8,128)S(1)}) custom-call(s32[64]{0:T(128)} %owners.1, bf16[128,512]{1,0:T(8,128)(2,1)} %q.1, bf16[128,512]{1,0:T(8,128)(2,1)} %do.1, bf16[128,256]{1,0:T(8,128)(2,1)} %k.1, bf16[128,256]{1,0:T(8,128)(2,1)} %v.1, ...), custom_call_target="tpu_custom_call" | custom-call | tf_op jit(solution)/shard_map/pallas_call | solution.py:560
  98.9 0.7 reduce_sum.30
  99.7 2.3 %convert_multiply_fusion = (f32[2048,256]{1,0:T(8,128)}, f32[2048,256]{1,0:T(8,128)}) fusion(bf16[2048,256]{1,0:T(8,128)(2,1)S(1)} %get-tuple-element.10, f32[256]{0:T(256)S(1)} %multiply_minimum_fusion, f32[256]{0:T(256)S(1)} %multiply_minimum_fusion.1, bf16[2048,256]{1,0:T(8,128)(2,1)S(1)} %get-tuple-element.8), kind=kLoop, calls=%fused_computation | loop fusion | flops 2097152 | bytes 6293504 | tf_op jit(solution)/shard_map/mul | solution.py:624
  (4 shorter events, 0.1 us)

commit v7 on v6

--- a/solution.py
+++ b/solution.py
@@ -25,6 +25,8 @@
 TILE = 256
 VMEM_BYTES = 55 * 1024 * 1024
 CHUNKS = 4
+SENDS = 24
+RECVS = 56
 ORDER = (3, 5, 4, 2, 6, 1, 7, 0)
 EPSILON = 1e-06
 NEGATIVE = -1e30
@@ -70,25 +72,56 @@
 
 class Copies:
     def __init__(self, send, recv):
-        self.send, self.recv, self.made = send, recv, []
-
-    def __call__(self, src, dst, device):
-        i = len(self.made)
+        self.send, self.recv, self.groups, self.slots = send, recv, [], 0
+
+    def group(self, region):
+        self.groups.append(region)
+        return len(self.groups) - 1
+
+    def slot(self):
+        self.slots += 1
+        return self.slots - 1
+
+    def start(self, src, dst, device, group, slot):
         copy = pltpu.make_async_remote_copy(
             src_ref=src,
             dst_ref=dst,
-            send_sem=self.send.at[i],
-            recv_sem=self.recv.at[i],
+            send_sem=self.send.at[group],
+            recv_sem=self.recv.at[slot],
             device_id=device,
             device_id_type=MESH,
         )
         copy.start()
-        self.made.append(copy)
         return copy
 
     def wait_sends(self):
-        for copy in self.made:
-            copy.wait_send()
+        for i, region in enumerate(self.groups):
+            take(region, self.send.at[i])
+
+
+def take(region, sem):
+    pltpu.make_async_copy(region, region, sem).wait()
+
+
+class Batch:
+    def __init__(self, copies, region, group=None):
+        self.copies, self.region = copies, region
+        self.group = copies.group(region) if group is None else group
+        self.slot = copies.slot()
+
+    def add(self, src, dst, device):
+        self.copies.start(src, dst, device, self.group, self.slot)
+
+    def wait_recv(self):
+        take(self.region, self.copies.recv.at[self.slot])
+
+
+class Chain:
+    def __init__(self, copies, region):
+        self.copies, self.group = copies, copies.group(region)
+
+    def __call__(self, src, dst, device):
+        return self.copies.start(src, dst, device, self.group, self.copies.slot())
 
 
 def greet(devices):
@@ -109,52 +142,57 @@
 def plane_ring(copies, p, src, where, rows):
     half = rows // 2
     right, left = p.xslot(1), p.xslot(-1)
-    far = p.xslot(2)
     partner = p.in_plane(p.xslot(0, True))
+    chain = Chain(copies, where(0, 0, (G - 1) * rows))
+    passed = Batch(copies, where(0, 0, X * rows), chain.group)
+
+    def hand(slot):
+        block = where(slot, 0, rows)
+        passed.add(block, block, partner)
+
     mine = where(p.slot, 0, rows)
-    a = copies(src, mine, p.in_plane(right))
-    b = copies(src, mine, p.in_plane(left))
-    own = copies(src, mine, partner)
+    a = chain(src, mine, p.in_plane(right))
+    b = chain(src, mine, p.in_plane(left))
+    passed.add(src, mine, partner)
     yield
     a.wait_recv()
     first = where(left, 0, half)
-    f = copies(first, first, p.in_plane(right))
-    block = where(left, 0, rows)
-    pa = copies(block, block, partner)
+    f = chain(first, first, p.in_plane(right))
+    hand(left)
     b.wait_recv()
     second = where(right, half, half)
-    g = copies(second, second, p.in_plane(left))
-    block = where(right, 0, rows)
-    pb = copies(block, block, partner)
+    g = chain(second, second, p.in_plane(left))
+    hand(right)
     yield
     f.wait_recv()
     g.wait_recv()
-    block = where(far, 0, rows)
-    pc = copies(block, block, partner)
+    hand(p.xslot(2))
     yield
-    own.wait_recv()
-    pa.wait_recv()
-    pb.wait_recv()
-    pc.wait_recv()
+    passed.wait_recv()
 
 
 def plane_direct(copies, p, src, where, rows):
     partner = p.in_plane(p.xslot(0, True))
+    chain = Chain(copies, where(0, 0, (G - 1) * rows))
+    passed = Batch(copies, where(0, 0, X * rows), chain.group)
+
+    def hand(slot):
+        block = where(slot, 0, rows)
+        passed.add(block, block, partner)
+
     mine = where(p.slot, 0, rows)
-    c, a, b = [copies(src, mine, p.in_plane(p.xslot(s))) for s in (2, 1, -1)]
-    passed = [copies(src, mine, partner)]
+    c, a, b = [chain(src, mine, p.in_plane(p.xslot(s))) for s in (2, 1, -1)]
+    passed.add(src, mine, partner)
     yield
-    for copy, s in ((a, -1), (b, 1)):
-        copy.wait_recv()
-        block = where(p.xslot(s), 0, rows)
-        passed.append(copies(block, block, partner))
+    a.wait_recv()
+    hand(p.xslot(-1))
+    b.wait_recv()
+    hand(p.xslot(1))
     yield
     c.wait_recv()
-    block = where(p.xslot(2), 0, rows)
-    passed.append(copies(block, block, partner))
+    hand(p.xslot(2))
     yield
-    for copy in passed:
-        copy.wait_recv()
+    passed.wait_recv()
 
 
 def whole(ref, rows):
@@ -166,17 +204,18 @@
         return ref.at[at(place(distance), TOK)]
 
     up, down = p.in_column(p.zslot(1)), p.in_column(p.zslot(-1))
-    u = copies(src, block(-1), up)
-    d = copies(src, block(1), down)
+    chain = Chain(copies, ref.at[pl.ds(0, (Z - 1) * TOK)])
+    u = chain(src, block(-1), up)
+    d = chain(src, block(1), down)
     for step in range(1, Z // 2 + 1):
         yield
         u.wait_recv()
         if step < Z // 2:
-            u = copies(block(-step), block(-step - 1), up)
+            u = chain(block(-step), block(-step - 1), up)
         if step < Z // 2:
             d.wait_recv()
             if step < Z // 2 - 1:
-                d = copies(block(step), block(step + 1), down)
+                d = chain(block(step), block(step + 1), down)
 
 
 def run(*rings):
@@ -367,7 +406,9 @@
         wsum[i] = jnp.broadcast_to(sum_squares(tw.at[i]), wsum.shape[1:])
     meet(everyone)
     copies = Copies(send, recv)
-    small = [copies(pg.at[p.slot], pg.at[p.slot], peer) for peer in plane_peers(p)]
+    small = Batch(copies, pg.at[pl.ds(0, G - 1)])
+    for peer in plane_peers(p):
+        small.add(pg.at[p.slot], pg.at[p.slot], peer)
     kr = column_ring(copies, p, own_k, kg)
     vr = column_ring(copies, p, own_v, vg)
     qr = plane_direct(copies, p, q, whole(qg, TOK), TOK)
@@ -376,18 +417,17 @@
         next(ring)
     for ring in (kr, vr):
         next(ring)
-    for copy in small:
-        copy.wait_recv()
+    small.wait_recv()
     build_bias(owners, pg, bias, p)
     for ring in (kr, vr, qr):
         next(ring)
     for ring in (kr, vr, dr, kr, vr, qr, dr):
         next(ring, None)
     run(qr, dr)
-    hs = []
+    hs = Batch(copies, hg.at[pl.ds(0, (G - 1) * TOK)])
     for s, f in ((2, False), (2, True), (1, False), (3, False), (1, True), (3, True), (0, True)):
         to = p.xslot(s, f)
-        hs.append(copies(strip(to), hg.at[mine], p.in_plane(to)))
+        hs.add(strip(to), hg.at[mine], p.in_plane(to))
     for load in loads[:5]:
         load.wait()
     kt[...] = kg[...].T
@@ -400,12 +440,12 @@
             pltpu.make_async_remote_copy(
                 src_ref=block,
                 dst_ref=block,
-                send_sem=share_send.at[n, t],
-                recv_sem=share_recv.at[n, t],
+                send_sem=share_send.at[0],
+                recv_sem=share_recv.at[t],
                 device_id=peer,
                 device_id_type=MESH,
             )
-            for n, peer in enumerate(peers)
+            for peer in peers
         ]
 
     def stats_step(t, carry):
@@ -418,28 +458,26 @@
     lax.fori_loop(0, tiles, stats_step, 0)
 
     def ready(t):
-        for copy in share(t):
-            copy.wait_recv()
+        take(shared.at[pl.ds(0, G - 1), :, tile_of(t)], share_recv.at[t])
         merge_stats(shared, tops, merged, t)
+
+    scattered = [Batch(copies, gz.at[i, pl.ds(0, Z - 1)]) for i in range(2)]
 
     def scatter(chunk):
         count = Z // CHUNKS
-        near = [s for s in FARTHEST if place(s) // count == chunk]
-        return [
-            [
-                copies(src.at[at(place(s), TOK)], gz.at[i, p.z], p.in_column(p.zslot(s)))
-                for s in near
-            ]
-            for i, src in enumerate((dk, dv))
-        ]
-
-    chunks = []
+        for i, src in enumerate((dk, dv)):
+            for s in FARTHEST:
+                if place(s) // count == chunk:
+                    scattered[i].add(
+                        src.at[at(place(s), TOK)], gz.at[i, p.z], p.in_column(p.zslot(s))
+                    )
+
     for chunk in range(CHUNKS):
         chunk_grads(
             qg, dog, kt, masses, dps, merged, probs, slopes, acc, dqt, dq, dk, dv, chunk,
             ready if chunk == 0 else lambda t: None,
         )
-        chunks.append(scatter(chunk))
+        scatter(chunk)
     own_g = [
         pltpu.make_async_copy(src.at[at(place(0), TOK)], gz.at[i, p.z], local.at[7 + i])
         for i, src in enumerate((dk, dv))
@@ -448,15 +486,14 @@
         load.start()
 
     def stream(i, raw):
-        made = [copy for parts in chunks for copy in parts[i]]
         own_g[i].wait()
-        for copy in made:
-            copy.wait_recv()
+        scattered[i].wait_recv()
         gy[i, p.y] = rounded_sum(gz, i, Z)
-        made = [copies(gy.at[i, p.y], gy.at[i, p.y], peer) for peer in row_peers(p)]
+        made = Batch(copies, gy.at[i, pl.ds(0, Y - 1)])
+        for peer in row_peers(p):
+            made.add(gy.at[i, p.y], gy.at[i, p.y], peer)
         yield
-        for copy in made:
-            copy.wait_recv()
+        made.wait_recv()
         for g in range(KVG):
             total = gy[i, g * members].astype(F32)
             for n in range(1, members):
@@ -468,22 +505,18 @@
         product = jnp.dot(hgt[...], grads[i], preferred_element_type=F32)
         part[i] = product.astype(BF16)
         rz[i, p.z] = part[i, at(p.z, piece), :]
-        made = [
-            copies(part.at[i, at(p.zslot(s), piece)], rz.at[i, p.z], p.in_column(p.zslot(s)))
-            for s in FARTHEST
-        ]
+        made = Batch(copies, rz.at[i, pl.ds(0, Z - 1)])
+        for s in FARTHEST:
+            made.add(part.at[i, at(p.zslot(s), piece)], rz.at[i, p.z], p.in_column(p.zslot(s)))
         yield
-        for copy in made:
-            copy.wait_recv()
+        made.wait_recv()
         own = at(p.z, piece)
         block[i, own, :] = rounded_sum(rz, i, Z)
-        made = [
-            copies(block.at[i, own], block.at[i, own], p.in_column(p.zslot(s)))
-            for s in FARTHEST
-        ]
+        made = Batch(copies, block.at[i, pl.ds(0, (Z - 1) * piece)])
+        for s in FARTHEST:
+            made.add(block.at[i, own], block.at[i, own], p.in_column(p.zslot(s)))
         yield
-        for copy in made:
-            copy.wait_recv()
+        made.wait_recv()
         ring = plane_ring(copies, p, block.at[i], whole(raw, wide), wide)
         next(ring)
         puts = [
@@ -494,52 +527,55 @@
         square = sum_squares(block.at[i])
         row = lax.broadcasted_iota(jnp.int32, (8, square.shape[1]), 0)
         ysum[i, p.y] = jnp.where(row == 0, square, wsum[i])
-        made = [copies(ysum.at[i, p.y], ysum.at[i, p.y], peer) for peer in row_peers(p)]
+        made = Batch(copies, ysum.at[i, pl.ds(0, Y - 1)])
+        for peer in row_peers(p):
+            made.add(ysum.at[i, p.y], ysum.at[i, p.y], peer)
         yield
         next(ring)
-        for copy in made:
-            copy.wait_recv()
+        made.wait_recv()
         total = ysum[i, 0]
         for n in range(1, Y):
             total = total + ysum[i, n]
         tot[i] = total
         puts[1].start()
-        made = [copies(tot.at[i], sums.at[i, p.slot], peer) for peer in plane_peers(p)]
+        made = Batch(copies, sums.at[i, pl.ds(0, G - 1)])
+        for peer in plane_peers(p):
+            made.add(tot.at[i], sums.at[i, p.slot], peer)
         yield
         next(ring)
         yield
         for _ in ring:
             pass
-        for copy in made:
-            copy.wait_recv()
+        made.wait_recv()
         for put in puts:
             put.wait()
 
     partner = p.in_plane(p.xslot(0, True))
-    given = [copies(dq.at[at(x * C + 1 - p.c, TOK)], pq.at[x], partner) for x in range(X)]
-    for copy in hs:
-        copy.wait_recv()
+    given = Batch(copies, pq)
+    for x in range(X):
+        given.add(dq.at[at(x * C + 1 - p.c, TOK)], pq.at[x], partner)
+    hs.wait_recv()
     hgt[...] = hg[...].T
     streams = [stream(0, raw_k), stream(1, raw_v)]
     for one in streams:
         next(one)
+    given.wait_recv()
     for x in range(X):
-        given[x].wait_recv()
         cq[x] = (dq[at(x * C + p.c, TOK), :].astype(F32) + pq[x].astype(F32)).astype(BF16)
-    qs = []
+    put_q = pltpu.make_async_copy(cq.at[p.x], dq_slots.at[p.x], local.at[13])
+    put_q.start()
+    for _ in range(3):
+        for one in streams:
+            next(one)
+    qs = Batch(copies, dq_slots.at[pl.ds(0, X - 1)])
     for s in (2, 1, 3):
         to = lax.rem(p.x + s, X)
-        qs.append(copies(cq.at[to], dq_slots.at[p.x], p.in_plane(to * C + p.c)))
-    put_q = pltpu.make_async_copy(cq.at[p.x], dq_slots.at[p.x], local.at[13])
-    put_q.start()
+        qs.add(cq.at[to], dq_slots.at[p.x], p.in_plane(to * C + p.c))
     run(*streams)
-    for copy in qs:
-        copy.wait_recv()
+    qs.wait_recv()
     put_q.wait()
     copies.wait_sends()
-    for t in range(tiles):
-        for copy in share(t):
-            copy.wait_send()
+    take(shared.at[pl.ds(0, G - 1)], share_send.at[0])
 
 
 def shape(dims, kind=BF16):
@@ -601,10 +637,10 @@
             pltpu.VMEM((2, model, columns), BF16),
             pltpu.VMEM((2, piece, columns), BF16),
             pltpu.VMEM((2, 8, columns), F32),
-            dma(180),
-            dma(180),
-            pltpu.SemaphoreType.DMA((G - 1, ROWS // TILE)),
-            pltpu.SemaphoreType.DMA((G - 1, ROWS // TILE)),
+            dma(SENDS),
+            dma(RECVS),
+            dma(1),
+            dma(ROWS // TILE),
             dma(14),
         ],
         compiler_params=pltpu.CompilerParams(

time: 102 us -> 96.4 us (0.945)
  Pallas kernels: 98.2 us -> 92.5 us
    pallas_call x1, Pallas kernels: 98.2 us -> 92.5 us  [local(): pl.pallas_call(kernel, out_shape=(pltpu.VMEM((X, TOK, width), BF16), pltp...]
where the time goes in v7:
time: 96.4 us; the launch traced here: 96.3 us
  Pallas kernels  92.5 us (96%)
  other arithmetic  3.15 us (3%)
    pallas_call x1, Pallas kernels, local(): pl.pallas_call(kernel, out_shape=(pltpu.VMEM((X, TOK, width), BF16), pltp...  92.5 us
    mul x1, other arithmetic, clipped(): return raw.astype(F32) * factor[None, :]  2.35 us

profile of v7, /device:TPU:1, one launch (start us, length us, event | category | flops | bytes accessed | tf_op | source)
XLA Modules:
  0.0 96.3 jit_solution(4821188763789083286)
XLA Ops:
  0.6 92.5 %shard_map.112 = (bf16[4,128,512]{2,1,0:T(8,128)(2,1)S(1)}, bf16[2048,256]{1,0:T(8,128)(2,1)S(1)}, bf16[2048,256]{1,0:T(8,128)(2,1)S(1)}, f32[2,8,8,256]{3,2,1,0:T(8,128)S(1)}) custom-call(s32[64]{0:T(128)} %owners.1, bf16[128,512]{1,0:T(8,128)(2,1)} %q.1, bf16[128,512]{1,0:T(8,128)(2,1)} %do.1, bf16[128,256]{1,0:T(8,128)(2,1)} %k.1, bf16[128,256]{1,0:T(8,128)(2,1)} %v.1, ...), custom_call_target="tpu_custom_call" | custom-call | tf_op jit(solution)/shard_map/pallas_call | solution.py:596
  93.1 0.7 reduce_sum.30
  94.0 2.3 %convert_multiply_fusion = (f32[2048,256]{1,0:T(8,128)}, f32[2048,256]{1,0:T(8,128)}) fusion(bf16[2048,256]{1,0:T(8,128)(2,1)S(1)} %get-tuple-element.10, f32[256]{0:T(256)S(1)} %multiply_minimum_fusion, f32[256]{0:T(256)S(1)} %multiply_minimum_fusion.1, bf16[2048,256]{1,0:T(8,128)(2,1)S(1)} %get-tuple-element.8), kind=kLoop, calls=%fused_computation | loop fusion | flops 2097152 | bytes 6293504 | tf_op jit(solution)/shard_map/mul | solution.py:660
  (4 shorter events, 0.1 us)
